TPU v7x, 256 devices: a whole 4x4x8 slice. The times are simulated.
256 devices in a mesh: expert: 8 (over x, core), hidden: 32 (over y, z).
Axes of the slice: x: 4, y: 4, z: 8, core: 2. Of those that a mesh axis runs over, the one named last changes fastest.
Arguments:
- tokens: bfloat16 [1024, 6144], P(('expert', 'hidden')), may hold values from -33 to 33
- norm_gain: float32 [6144], replicated, may hold values from 0.1 to 1.9
- gate_weight: bfloat16 [8, 6144, 8192], P('expert', None, 'hidden'), may hold values from -0.078125 to 0.078125
- up_weight: bfloat16 [8, 6144, 8192], P('expert', None, 'hidden'), may hold values from -0.078125 to 0.078125
- down_weight: bfloat16 [8, 8192, 6144], P('expert', 'hidden'), may hold values from -0.125 to 0.125
- expert_ids: int32 [1024, 2], P('expert'), may hold values from 0 to 7, all different within a row; in each aligned block of 4 rows (0 to 3, 4 to 7, ...) at most 2 rows name the same one
- route_weight: float32 [1024, 2], P('expert'), may hold values from 0.2 to 1
Outputs:
- settled_state: bfloat16 [1024, 6144], P(('expert', 'hidden'))
Inputs may be any that keep to these rules, and one draw needn't show every extreme that they name: `expert_ids`: in each aligned block of 4 rows (the tokens of one device) the two ids of a row differ and no expert is named more than 2 times; some expert is named exactly 2 times.
All inputs are finite; a program needn't handle non-finite values.
Results may differ from a plain program's by a relative error of at most 0.0085.
Values may be sent and summed in bfloat16 or wider, within the bound.
No kernel may reach another device: no remote copies, remote signals or barrier semaphores. Data moves between devices by JAX's collectives and lax.ppermute only.
A program may use at most 64 MiB of HBM per device.

v0:
```python
import jax
import jax.numpy as jnp
from jax import lax
from jax.sharding import PartitionSpec as P

ITERS = 2


EPSILON = 1e-05
NUDGE = 0.5


def rms_norm(values, norm_gain):
    widened = values.astype(jnp.float32)
    mean_square = jnp.mean(widened * widened, axis=-1, keepdims=True)
    return (widened * lax.rsqrt(mean_square + EPSILON) * norm_gain).astype(jnp.bfloat16)


def slot_table(id_blocks, experts, capacity):
    groups = id_blocks.shape[0]
    tok_count = id_blocks.shape[1]
    flat_ids = id_blocks.reshape(groups, tok_count * 2)
    expert_range = jnp.arange(experts, dtype=jnp.int32)
    one_hot = (flat_ids[:, :, None] == expert_range[None, None, :]).astype(jnp.int32)
    before = jnp.cumsum(one_hot, axis=1) - one_hot
    within = jnp.sum(before * one_hot, axis=2)
    return (flat_ids * capacity + within).reshape(groups, tok_count, 2)


def dispatch(token_block, slots, slot_count):
    groups = token_block.shape[0]
    tok_count = token_block.shape[1]
    width = token_block.shape[2]
    token_index = jnp.broadcast_to(
        jnp.arange(tok_count, dtype=jnp.int32)[None, :, None], slots.shape
    )
    group_index = jnp.broadcast_to(jnp.arange(groups, dtype=jnp.int32)[:, None, None], slots.shape)
    source = (
        jnp.full((groups, slot_count), tok_count, jnp.int32).at[group_index, slots].set(token_index)
    )
    padded = jnp.concatenate(
        [token_block, jnp.zeros((groups, 1, width), token_block.dtype)], axis=1
    )
    return jax.vmap(lambda table_rows, chosen: jnp.take(table_rows, chosen, axis=0))(padded, source)


def expert_partial(inputs, gate_weight, up_weight, down_weight):
    gate_value = jnp.dot(inputs, gate_weight[0], preferred_element_type=jnp.float32)
    up_value = jnp.dot(inputs, up_weight[0], preferred_element_type=jnp.float32)
    hidden_units = (jax.nn.silu(gate_value) * up_value).astype(jnp.bfloat16)
    return jnp.dot(hidden_units, down_weight[0], preferred_element_type=jnp.float32)


def on_device(tokens, norm_gain, gate_weight, up_weight, down_weight, expert_ids, route_weight):
    experts = lax.axis_size("expert")
    tok_count = tokens.shape[0]
    capacity = tok_count // 2
    slot_count = experts * capacity
    position = lax.axis_index("hidden")
    own_ids = lax.dynamic_slice_in_dim(expert_ids, position * tok_count, tok_count, 0)
    own_weights = lax.dynamic_slice_in_dim(route_weight, position * tok_count, tok_count, 0)
    own_slots = slot_table(own_ids[None], experts, capacity)[0]
    state = tokens
    for iteration in range(ITERS):
        normed = rms_norm(state, norm_gain)
        outgoing = dispatch(normed[None], own_slots[None], slot_count)[0]
        arrived = lax.all_to_all(outgoing, "expert", split_axis=0, concat_axis=0, tiled=True)
        gathered = lax.all_gather(arrived, "hidden", axis=0, tiled=True)
        partials = expert_partial(gathered, gate_weight, up_weight, down_weight)
        summed = lax.psum_scatter(
            partials.astype(jnp.bfloat16), "hidden", scatter_dimension=0, tiled=True
        )
        returned = lax.all_to_all(summed, "expert", split_axis=0, concat_axis=0, tiled=True)
        first = (
            jnp.take(returned, own_slots[:, 0], axis=0).astype(jnp.float32) * own_weights[:, 0:1]
        )
        second = (
            jnp.take(returned, own_slots[:, 1], axis=0).astype(jnp.float32) * own_weights[:, 1:2]
        )
        mixed = first + second
        state = (
            NUDGE * state.astype(jnp.float32) + NUDGE * (tokens.astype(jnp.float32) + mixed)
        ).astype(jnp.bfloat16)
    return state


def solution(mesh):
    placed = (
        P(("expert", "hidden"), None),
        P(),
        P("expert", None, "hidden"),
        P("expert", None, "hidden"),
        P("expert", "hidden", None),
        P("expert", None),
        P("expert", None),
    )
    return jax.shard_map(
        on_device,
        mesh=mesh,
        in_specs=placed,
        out_specs=P(("expert", "hidden"), None),
        check_vma=False,
    )
```

profile of v0, /device:TPU:1, one launch (start us, length us, event | category | flops | bytes accessed | tf_op | source)
XLA Modules:
  0.0 718.7 jit_solution(2852176084333791114)
XLA Ops:
  6.5 0.9 constant_dynamic-slice_fusion.1
  7.4 0.1 copy.20
  7.6 0.1 reshape.242
  7.8 0.2 select_reduce_fusion
  8.1 0.1 copy.17
  8.2 0.1 copy.19
  8.4 0.6 scatter_custom_fusion
  9.0 1.0 fusion.27
  10.0 0.9 fusion.32
  11.0 1.1 gather_fusion
  12.1 0.1 bitcast_select_fusion.1
  12.2 0.1 all_to_all.32
  12.3 11.5 %all_to_all.48 = bf16[8,2,6144]{2,1,0:T(2,128)(2,1)S(1)} all-to-all(bf16[8,2,6144]{2,1,0:T(2,128)(2,1)S(1)} %all_to_all.32), channel_id=1, replica_groups=mesh['expert'=8,'hidden'=32] {'expert'}, dimensions={0} | all-to-all | bytes 393216 | tf_op jit(solution)/shard_map/all_to_all | solution.py:67
  23.9 0.8 all_to_all.34
  24.7 89.8 %all-gather.3.cloned.1.call-done = bf16[512,6144]{1,0:T(8,128)(2,1)} async-done(((bf16[16,6144]{1,0:T(8,128)(2,1)}), bf16[512,6144]{1,0:T(8,128)(2,1)}) %all-gather.3.cloned.1.call-update) | async-done | bytes 6291472 | tf_op jit(solution)/shard_map/all_gather | solution.py:68
  114.5 5.6 fusion.8
  120.2 0.7 copy-done.7
  120.9 1.8 fusion.19
  122.7 4.5 convolution_convert_fusion.1
  127.2 0.7 copy-done.4
  128.0 0.2 slice_reduce_fusion.1
  128.2 0.5 compare_and_fusion
  128.7 217.0 %reduce-scatter.3.cloned.1.call-done = bf16[16,6144]{1,0:T(8,128)(2,1)} async-done(((bf16[512,6144]{1,0:T(8,128)(2,1)}), bf16[16,6144]{1,0:T(8,128)(2,1)}) %reduce-scatter.3.cloned.1.call-update) | async-done | bytes 196624 | tf_op jit(solution)/shard_map/reduce_scatter | solution.py:70
  345.7 1.7 all_to_all.35
  347.4 8.9 %all-to-all-start.1 = ((bf16[8,2,6144]{2,1,0:T(2,128)(2,1)}), bf16[8,2,6144]{2,1,0:T(2,128)(2,1)S(1)}, u32[]{:S(2)}, u32[]{:S(2)}) async-start(bf16[8,2,6144]{2,1,0:T(2,128)(2,1)} %all_to_all.35), calls=%async_computation.2 | async-start | bytes 393216 | tf_op jit(solution)/shard_map/all_to_all | solution.py:73
  356.3 0.5 slice_bitcast_fusion.1
  356.8 5.3 all-to-all-done.1
  362.3 0.6 gather_fusion.2
  362.9 0.6 gather_fusion.1
  363.5 1.1 fusion.22
  364.6 0.8 fusion.33
  365.5 1.1 gather_fusion.3
  366.6 0.8 bitcast_select_fusion
  367.3 0.1 all_to_all.38
  367.5 9.2 %all_to_all.49 = bf16[8,2,6144]{2,1,0:T(2,128)(2,1)S(1)} all-to-all(bf16[8,2,6144]{2,1,0:T(2,128)(2,1)S(1)} %all_to_all.38), channel_id=1, replica_groups=mesh['expert'=8,'hidden'=32] {'expert'}, dimensions={0} | all-to-all | bytes 393216 | tf_op jit(solution)/shard_map/all_to_all | solution.py:67
  376.7 0.8 all_to_all.40
  377.5 0.2 reduce-scatter.5.cloned.1.call-start
  377.7 84.9 %all-gather.5.cloned.1.call-done = bf16[512,6144]{1,0:T(8,128)(2,1)} async-done(((bf16[16,6144]{1,0:T(8,128)(2,1)}), bf16[512,6144]{1,0:T(8,128)(2,1)}) %all-gather.5.cloned.1.call-update) | async-done | bytes 6291472 | tf_op jit(solution)/shard_map/all_gather | solution.py:68
  462.7 5.6 fusion.6
  468.3 0.8 copy-done.8
  469.1 1.8 fusion.16
  470.9 4.5 convolution_convert_fusion
  475.4 217.8 %reduce-scatter.5.cloned.1.call-done = bf16[16,6144]{1,0:T(8,128)(2,1)} async-done(((bf16[512,6144]{1,0:T(8,128)(2,1)}), bf16[16,6144]{1,0:T(8,128)(2,1)}) %reduce-scatter.5.cloned.1.call-update) | async-done | bytes 196624 | tf_op jit(solution)/shard_map/reduce_scatter | solution.py:70
  693.2 1.1 all_to_all.41
  694.2 15.1 %all_to_all.50 = bf16[8,2,6144]{2,1,0:T(2,128)(2,1)S(1)} all-to-all(bf16[8,2,6144]{2,1,0:T(2,128)(2,1)S(1)} %all_to_all.41), channel_id=1, replica_groups=mesh['expert'=8,'hidden'=32] {'expert'}, dimensions={0} | all-to-all | bytes 393216 | tf_op jit(solution)/shard_map/all_to_all | solution.py:73
  709.4 0.6 gather_fusion.5
  710.0 0.6 gather_fusion.4
  710.6 1.6 fusion.26
  (45 shorter events, 0.8 us)
Async XLA Ops:
  6.5 116.2 %copy-start = (bf16[1,256,6144]{2,1,0:T(8,128)(2,1)S(1)}, bf16[1,256,6144]{2,1,0:T(8,128)(2,1)}, u32[]{:S(2)}) copy-start(bf16[1,256,6144]{2,1,0:T(8,128)(2,1)} %param.15) | copy-start | bytes 9437188
  6.5 108.0 %all-gather.3.cloned.1.call-start = ((), (), s32[]{:S(2)}) async-start(), calls=%async_computation.6 | async-start | bytes 6488064 | tf_op jit(solution)/shard_map/all_gather | solution.py:68
  9.0 111.2 %copy-start.3 = (pred[16]{0:T(512)(128)(4,1)}, pred[16]{0:T(512)(128)(4,1)S(1)}, u32[]{:S(2)}) copy-start(pred[16]{0:T(512)(128)(4,1)S(1)} %and_bitcast_fusion) | copy-start | bytes 52
  24.6 321.0 %reduce-scatter.3.cloned.1.call-start = ((), (), s32[]{:S(2)}) async-start(), calls=%async_computation.7 | async-start | bytes 6488064 | tf_op jit(solution)/shard_map/reduce_scatter | solution.py:70
  114.5 5.7 copy-start.5
  114.5 6.4 copy-start.7
  127.2 0.7 copy-start.4
  347.4 14.8 %all-to-all-start.1 = ((bf16[8,2,6144]{2,1,0:T(2,128)(2,1)}), bf16[8,2,6144]{2,1,0:T(2,128)(2,1)S(1)}, u32[]{:S(2)}, u32[]{:S(2)}) async-start(bf16[8,2,6144]{2,1,0:T(2,128)(2,1)} %all_to_all.35), calls=%async_computation.2 | async-start | bytes 393216 | tf_op jit(solution)/shard_map/all_to_all | solution.py:73
  356.3 106.4 %all-gather.5.cloned.1.call-start = ((), (), s32[]{:S(2)}) async-start(), calls=%async_computation.8 | async-start | bytes 6488064 | tf_op jit(solution)/shard_map/all_gather | solution.py:68
  364.6 0.9 copy-start.1
  377.5 315.6 %reduce-scatter.5.cloned.1.call-start = ((), (), s32[]{:S(2)}) async-start(), calls=%async_computation.9 | async-start | bytes 6488064 | tf_op jit(solution)/shard_map/reduce_scatter | solution.py:70
  462.7 5.7 copy-start.6
  462.7 6.4 copy-start.8
  475.4 235.2 %copy-start.2 = (pred[4]{0:T(512)(128)(4,1)S(1)}, pred[4]{0:T(512)(128)(4,1)}, u32[]{:S(2)}) copy-start(pred[4]{0:T(512)(128)(4,1)} %get-tuple-element.18) | copy-start | bytes 16
Sparse Core Ops, SparseCore 0:
  24.8 89.7 all-gather.2
  127.3 218.2 reduce-scatter.2
  377.6 85.0 all-gather.4
  475.5 217.5 reduce-scatter.4
where the time goes:
time: 719 us
  waiting for transfers between devices  615 us (86%)
  blocking collectives  35.8 us (5%)
  matrix products  23.8 us (3%)
  local copies, waits for them, and re-layouts  14.6 us (2%)
  between operations  13.4 us (2%)
  starting transfers between devices  9.15 us (1%)
    reduce_scatter x2, waiting for transfers between devices, on_device(): lax.psum_scatter(partials.astype(jnp.bfloat16), 'hidden', scatter_dimensi...  435 us
    all_gather x2, waiting for transfers between devices, on_device(): gathered = lax.all_gather(arrived, 'hidden', axis=0, tiled=True)  175 us
    all_to_all x2, blocking collectives, on_device(): lax.all_to_all(outgoing, 'expert', split_axis=0, concat_axis=0, tiled=True)  20.8 us
    all_to_all x1, blocking collectives, on_device(): lax.all_to_all(summed, 'expert', split_axis=0, concat_axis=0, tiled=True)  15.1 us
  transfers between devices with their start and end apart: 5, of which 5 were waited for; matrix products, arithmetic and copies ran while one was open for 0% of the time, Pallas kernels for 0%

commit v1 on v0

v1 whole, which is shorter than its diff:
```python
import jax
import jax.numpy as jnp
from jax import lax
from jax.experimental import pallas as pl
from jax.experimental.pallas import tpu as pltpu
from jax.sharding import PartitionSpec as P

ITERS = 2
EPSILON = 1e-05
NUDGE = 0.5
RING = 4

BF16 = jnp.bfloat16
F32 = jnp.float32


def row_groups(hidden):
    depth = hidden // RING
    across = [[y * depth + z for y in range(RING)] for z in range(depth)]
    along = [[y * depth + z for z in range(depth)] for y in range(RING)]
    return across, along


def home_groups(experts, hidden):
    depth = hidden // RING
    return [
        [e * hidden + y * depth + z for e in range(experts) for y in range(RING)]
        for z in range(depth)
    ]


def rms_norm(values, norm_gain):
    widened = values.astype(F32)
    mean_square = jnp.mean(widened * widened, axis=-1, keepdims=True)
    return (widened * lax.rsqrt(mean_square + EPSILON) * norm_gain).astype(BF16)


def routing(ids, weights, slot_count, capacity):
    tok_count = ids.shape[0]
    flat = ids.reshape(-1)
    order = jnp.arange(flat.shape[0], dtype=jnp.int32)
    earlier = (flat[:, None] == flat[None, :]) & (order[None, :] < order[:, None])
    within = jnp.sum(earlier.astype(jnp.int32), axis=1)
    slots = (flat * capacity + within).reshape(tok_count, 2)
    hits = slots[:, :, None] == jnp.arange(slot_count, dtype=jnp.int32)[None, None, :]
    send = jnp.sum(hits.astype(F32), axis=1).astype(BF16)
    mix = jnp.sum(jnp.where(hits, weights[:, :, None], 0.0), axis=1)
    return send, mix


def exchange(values, axis, groups):
    return lax.all_to_all(values, axis, 0, 0, tiled=True, axis_index_groups=groups)


def spread(values, copies, axis, groups):
    return exchange(jnp.broadcast_to(values[None], (copies,) + values.shape), axis, groups)


def shifts(hidden, step, ring):
    depth = hidden // RING
    if ring == "along":
        return [(i, (i // depth) * depth + (i % depth + step) % depth) for i in range(hidden)]
    return [(i, ((i // depth + step) % RING) * depth + i % depth) for i in range(hidden)]


def shift(values, hidden, step, ring):
    return lax.ppermute(values, "hidden", shifts(hidden, step, ring))


def ring_gather(own, hidden):
    half = own.shape[0] // 2
    up, down = own, own
    blocks = {0: own}
    for step in range(1, 4):
        up, down = shift(up, hidden, 1, "along"), shift(down, hidden, -1, "along")
        blocks[-step], blocks[step] = up, down
    blocks[4] = jnp.concatenate(
        [shift(up[:half], hidden, 1, "along"), shift(down[half:], hidden, -1, "along")]
    )
    return blocks


def ring_sum(blocks, far, hidden, ring):
    half = blocks[0].shape[0] // 2
    wide = {k: v.astype(F32) for k, v in blocks.items()}
    up = shift(blocks[far][:half], hidden, 1, ring).astype(F32)
    down = shift(blocks[far][half:], hidden, -1, ring).astype(F32)
    for step in range(far - 1, 0, -1):
        right, left = wide[step], wide[-step]
        if step == far - 1:
            right = jnp.concatenate([right[:half] + up, right[half:]])
            left = jnp.concatenate([left[:half], left[half:] + down])
        else:
            right, left = right + up, left + down
        up = shift(right.astype(BF16), hidden, 1, ring).astype(F32)
        down = shift(left.astype(BF16), hidden, -1, ring).astype(F32)
    return wide[0] + up + down


def feature_part(weight, position, hidden, step):
    depth = hidden // RING
    part = weight.shape[0] // RING
    start = lax.rem(position // depth + step, RING) * part
    rows = lax.dynamic_slice_in_dim(weight, start, part, 0)
    return shift(rows, hidden, step, "across") if step else rows


def hold(values):
    return pltpu.with_memory_space_constraint(values, pltpu.HBM)


def whole_block():
    return pl.BlockSpec(memory_space=pltpu.VMEM)


def params(mib):
    return pltpu.CompilerParams(
        dimension_semantics=("arbitrary",), vmem_limit_bytes=mib * 1024 * 1024
    )


def silu_product(gate_value, up_value):
    return (gate_value / (1.0 + jnp.exp(-gate_value)) * up_value).astype(BF16)


def whole_gate_up(rows, gate, up):
    count, width = rows.shape
    units = gate.shape[1]
    depth = width // 6

    def kernel(rows_ref, gate_ref, up_ref, out_ref, gate_sum, up_sum):
        step = pl.program_id(0)
        block = rows_ref[...]
        features = pl.ds(pl.multiple_of(step * depth, depth), depth)
        gate_part = jnp.dot(block, gate_ref[features, :], preferred_element_type=F32)
        up_part = jnp.dot(block, up_ref[features, :], preferred_element_type=F32)

        @pl.when(step == 0)
        def _():
            gate_sum[...] = gate_part
            up_sum[...] = up_part

        @pl.when(step > 0)
        def _():
            gate_sum[...] += gate_part
            up_sum[...] += up_part

        @pl.when(step == pl.num_programs(0) - 1)
        def _():
            out_ref[...] = silu_product(gate_sum[...], up_sum[...])

    return pl.pallas_call(
        kernel,
        grid=(width // depth,),
        in_specs=[
            pl.BlockSpec((count, depth), lambda k: (0, k)),
            whole_block(),
            whole_block(),
        ],
        out_specs=pl.BlockSpec((count, units), lambda k: (0, 0)),
        out_shape=jax.ShapeDtypeStruct((count, units), BF16),
        scratch_shapes=[pltpu.VMEM((count, units), F32), pltpu.VMEM((count, units), F32)],
        compiler_params=params(24),
        cost_estimate=pl.CostEstimate(
            flops=4 * count * width * units,
            bytes_accessed=2 * (count * width + 2 * width * units),
            transcendentals=count * units,
        ),
    )(hold(rows), gate, up)


def part_gate_up(rows, gate, up_parts, place):
    count, part = rows.shape
    units = gate.shape[1]

    def kernel(place_ref, rows_ref, gate_ref, up_ref, out_ref):
        block = rows_ref[...]
        out_ref[:, :units] = jnp.dot(block, gate_ref[...], preferred_element_type=F32).astype(BF16)
        up = up_ref[place_ref[0]]
        out_ref[:, units:] = jnp.dot(block, up, preferred_element_type=F32).astype(BF16)

    return pl.pallas_call(
        kernel,
        in_specs=[pl.BlockSpec(memory_space=pltpu.SMEM)] + [whole_block()] * 3,
        out_specs=whole_block(),
        out_shape=jax.ShapeDtypeStruct((count, 2 * units), BF16),
        compiler_params=pltpu.CompilerParams(vmem_limit_bytes=8 * 1024 * 1024),
        cost_estimate=pl.CostEstimate(
            flops=4 * count * part * units,
            bytes_accessed=2 * (count * part + 2 * part * units + count * units * 2),
            transcendentals=0,
        ),
    )(place, rows, gate, up_parts)


def down_product(gathered, down_parts):
    ring, count, units = gathered.shape
    part = down_parts.shape[2]
    columns = part // 3

    def kernel(rows_ref, down_ref, out_ref):
        total = jnp.dot(rows_ref[0], down_ref[0], preferred_element_type=F32)
        for y in range(1, ring):
            total = total + jnp.dot(rows_ref[y], down_ref[y], preferred_element_type=F32)
        out_ref[...] = total.astype(BF16)

    return pl.pallas_call(
        kernel,
        grid=(part // columns,),
        in_specs=[whole_block(), pl.BlockSpec((ring, units, columns), lambda n: (0, 0, n))],
        out_specs=pl.BlockSpec((count, columns), lambda n: (0, n)),
        out_shape=jax.ShapeDtypeStruct((count, part), BF16),
        compiler_params=params(16),
        cost_estimate=pl.CostEstimate(
            flops=2 * count * part * units * ring,
            bytes_accessed=2 * (ring * count * units + ring * units * part + count * part),
            transcendentals=0,
        ),
    )(gathered, down_parts)


def on_device(tokens, norm_gain, gate_weight, up_weight, down_weight, expert_ids, route_weight):
    experts = lax.axis_size("expert")
    hidden = lax.axis_size("hidden")
    depth = hidden // RING
    tok_count, width = tokens.shape
    part = width // RING
    units = gate_weight.shape[2]
    capacity = tok_count // 2
    slot_count = experts * capacity
    block = RING * slot_count
    across, along = row_groups(hidden)
    homes = home_groups(experts, hidden)
    both = ("expert", "hidden")

    position = lax.axis_index("hidden")
    own_ids = lax.dynamic_slice_in_dim(expert_ids, position * tok_count, tok_count, 0)
    own_weights = lax.dynamic_slice_in_dim(route_weight, position * tok_count, tok_count, 0)
    send, mix = routing(own_ids, own_weights, slot_count, capacity)

    def outgoing(state):
        normed = rms_norm(state, norm_gain)
        return jnp.einsum("ts,td->sd", send, normed, preferred_element_type=F32).astype(BF16)

    def finish(units_of, down_parts):
        return down_product(spread(units_of, RING, "hidden", across), down_parts)

    def settle(summed, state):
        returned = exchange(summed.astype(BF16).reshape(experts * RING, capacity, part), both, homes)
        returned = returned.reshape(experts, RING, capacity, part).astype(F32)
        mixed = jnp.einsum(
            "tec,eycd->tyd",
            mix.reshape(tok_count, experts, capacity),
            returned,
            precision=lax.Precision.HIGHEST,
        ).reshape(tok_count, width)
        return (
            NUDGE * state.astype(F32) + NUDGE * (tokens.astype(F32) + mixed)
        ).astype(BF16)

    rows = outgoing(tokens).reshape(experts, 1, capacity, width)
    rows = jnp.broadcast_to(rows, (experts, RING, capacity, width))
    rows = exchange(rows.reshape(experts * RING, capacity, width), both, homes)
    rows = rows.reshape(block, width)
    gate, up, down = gate_weight[0], up_weight[0], down_weight[0]
    near = [feature_part(gate, position, hidden, step) for step in (1, 3)]
    rows, down_in = lax.optimization_barrier((rows, down))
    gathered = lax.all_gather(rows, "hidden", axis=0, tiled=True, axis_index_groups=along)
    down_parts = exchange(
        down_in.reshape(units, RING, part).transpose(1, 0, 2), "hidden", across
    )
    gathered, near, down_parts = lax.optimization_barrier((gathered, near, down_parts))
    partial = finish(whole_gate_up(gathered, gate, up), down_parts)
    partial, up_in = lax.optimization_barrier((partial, up))
    up_parts = [feature_part(up_in, position, hidden, step) for step in range(RING)]
    summed = lax.psum_scatter(
        partial, "hidden", scatter_dimension=0, tiled=True, axis_index_groups=along
    )
    up_parts = exchange(up_in.reshape(RING, part, units), "hidden", across)
    summed, up_parts = lax.optimization_barrier((summed, up_parts))
    state = settle(summed, tokens)

    rows = outgoing(state).reshape(experts, capacity, RING, part).transpose(0, 2, 1, 3)
    rows = exchange(rows.reshape(experts * RING, capacity, part), both, homes)
    rows, gate_in = lax.optimization_barrier((rows, gate))
    far = [feature_part(gate_in, position, hidden, step) for step in (0, 2)]
    gate_parts = [far[0], near[0], far[1], near[1]]
    blocks = ring_gather(rows.reshape(block, part), hidden)
    offsets = sorted(blocks)
    gathered = jnp.concatenate([blocks[step] for step in offsets])
    gathered, gate_parts = lax.optimization_barrier((gathered, gate_parts))
    values = {
        step: part_gate_up(
            gathered,
            gate_parts[-step % RING],
            up_parts,
            lax.rem(position // depth + step + RING, RING).reshape(1),
        )
        for step in (2, 1, -1, 0)
    }
    values = ring_sum(values, 2, hidden, "across")
    partial = finish(silu_product(values[:, :units], values[:, units:]), down_parts)
    blocks = {
        step: partial[place * block : (place + 1) * block] for place, step in enumerate(offsets)
    }
    return settle(ring_sum(blocks, 4, hidden, "along"), state)


def solution(mesh):
    placed = (
        P(("expert", "hidden"), None),
        P(),
        P("expert", None, "hidden"),
        P("expert", None, "hidden"),
        P("expert", "hidden", None),
        P("expert", None),
        P("expert", None),
    )
    return jax.shard_map(
        on_device,
        mesh=mesh,
        in_specs=placed,
        out_specs=P(("expert", "hidden"), None),
        check_vma=False,
    )
```

time: 719 us -> 354 us (0.49)
  waiting for transfers between devices: 615 us -> 121 us
  blocking collectives: 35.8 us -> 106 us
  starting transfers between devices: 9.15 us -> 50.5 us
  matrix products: 23.8 us -> 3.46 us
  Pallas kernels: 0 us -> 20.1 us
  local copies, waits for them, and re-layouts: 14.6 us -> 32.7 us
    reduce_scatter x2 -> x1, waiting for transfers between devices: 435 us -> 0.01 us  [on_device(): lax.psum_scatter(partial, 'hidden', scatter_dimension=0, tiled=True, axis...]
    all_gather x2 -> x1, waiting for transfers between devices: 175 us -> 12 us  [on_device(): lax.all_gather(rows, 'hidden', axis=0, tiled=True, axis_index_groups=along)]
    ppermute x0 -> x23, waiting for transfers between devices: none -> 90.6 us  [shift(): return lax.ppermute(values, 'hidden', shifts(hidden, step, ring))]
    all_to_all x3 -> x5, blocking collectives: 35.8 us -> 106 us  [exchange(): lax.all_to_all(values, axis, 0, 0, tiled=True, axis_index_groups=groups)]
    ppermute x0 -> x23, starting transfers between devices: none -> 29.4 us  [shift(): return lax.ppermute(values, 'hidden', shifts(hidden, step, ring))]
    dot_general x6 -> x4, matrix products: 23.8 us -> 3.46 us  [the longest x2 2.08 us: outgoing(): jnp.einsum('ts,td->sd', send, normed, preferred_element_type=F32)]
    pallas_call x0 -> x7, Pallas kernels: none -> 20.1 us  [the longest x2 8.89 us: down_product(): pl.pallas_call(kernel, grid=(part // columns,), in_specs=[whole_block(),...]
    unnamed x19 -> x44, local copies, waits for them, and re-layouts: 2.28 us -> 16.8 us
  transfers between devices with their start and end apart: 5 -> 28, of which waited for: 5 -> 18; matrix products, arithmetic and copies ran while one was open for 0% -> 4% of each run, Pallas kernels for 0% -> 1%
where the time goes in v1:
time: 354 us; the launch traced here: 352 us
  waiting for transfers between devices  121 us (34%)
  blocking collectives  106 us (30%)
  starting transfers between devices  50.5 us (14%)
  local copies, waits for them, and re-layouts  32.7 us (9%)
  Pallas kernels  20.1 us (6%)
  between operations  13.9 us (4%)
  other arithmetic  5 us (1%)
    all_to_all x5, blocking collectives, exchange(): lax.all_to_all(values, axis, 0, 0, tiled=True, axis_index_groups=groups)  106 us
    ppermute x23, waiting for transfers between devices, shift(): return lax.ppermute(values, 'hidden', shifts(hidden, step, ring))  90.6 us
    ppermute x23, starting transfers between devices, shift(): return lax.ppermute(values, 'hidden', shifts(hidden, step, ring))  29.4 us
    all_to_all x3, starting transfers between devices, exchange(): lax.all_to_all(values, axis, 0, 0, tiled=True, axis_index_groups=groups)  21.1 us
    all_to_all x3, waiting for transfers between devices, exchange(): lax.all_to_all(values, axis, 0, 0, tiled=True, axis_index_groups=groups)  18.4 us
    unnamed x44, local copies, waits for them, and re-layouts  16.8 us
    all_gather x1, waiting for transfers between devices, on_device(): lax.all_gather(rows, 'hidden', axis=0, tiled=True, axis_index_groups=along)  12 us
    pallas_call x2, Pallas kernels, down_product(): pl.pallas_call(kernel, grid=(part // columns,), in_specs=[whole_block(),...  8.89 us
  transfers between devices with their start and end apart: 28, of which 18 were waited for; matrix products, arithmetic and copies ran while one was open for 4% of the time, Pallas kernels for 1%

profile of v1, /device:TPU:1, one launch (start us, length us, event | category | flops | bytes accessed | tf_op | source)
XLA Modules:
  0.0 352.4 jit_solution(1099390013597440749)
XLA Ops:
  10.9 1.4 broadcast_in_dim.23
  12.3 8.6 %all-to-all-start = ((bf16[32,2,6144]{2,1,0:T(2,128)(2,1)}), bf16[32,2,6144]{2,1,0:T(2,128)(2,1)}, u32[]{:S(2)}, u32[]{:S(2)}) async-start(bf16[32,2,6144]{2,1,0:T(2,128)(2,1)} %bitcast.1), calls=%async_computation | async-start | bytes 1572864 | tf_op jit(solution)/shard_map/all_to_all | solution.py:52
  21.0 3.2 copy.27
  24.1 10.4 %all-to-all-done = bf16[32,2,6144]{2,1,0:T(2,128)(2,1)} async-done(((bf16[32,2,6144]{2,1,0:T(2,128)(2,1)}), bf16[32,2,6144]{2,1,0:T(2,128)(2,1)}, u32[]{:S(2)}, u32[]{:S(2)}) %all-to-all-start) | async-done | bytes 786464 | tf_op jit(solution)/shard_map/all_to_all | solution.py:52
  34.5 3.0 reshape.88
  37.5 2.9 copy.28
  40.3 4.6 %all-to-all-start.1 = ((bf16[4,256,1536]{2,1,0:T(8,128)(2,1)}), bf16[4,256,1536]{2,1,0:T(8,128)(2,1)}, u32[]{:S(2)}, u32[]{:S(2)}) async-start(bf16[4,256,1536]{2,1,0:T(8,128)(2,1)} %bitcast.6), calls=%async_computation.1 | async-start | bytes 6291456 | tf_op jit(solution)/shard_map/all_to_all | solution.py:52
  45.1 1.6 dynamic-slice_bitcast_fusion
  46.7 1.4 collective-permute-start
  49.5 48.6 %collective-permute-done.gate_ref = bf16[1536,256]{1,0:T(8,128)(2,1)S(1)} collective-permute-done((bf16[1536,256]{1,0:T(8,128)(2,1)S(1)}, bf16[1536,256]{1,0:T(8,128)(2,1)S(1)}, u32[]{:S(2)}, u32[]{:S(2)}) %collective-permute-start) | collective-permute-done | bytes 786464 | tf_op jit(solution)/shard_map/ppermute | solution.py:67
  99.9 12.0 %all-gather.2.cloned.1.call-done.rows_ref = bf16[512,6144]{1,0:T(8,128)(2,1)} async-done(((bf16[64,6144]{1,0:T(8,128)(2,1)}), bf16[512,6144]{1,0:T(8,128)(2,1)}) %all-gather.2.cloned.1.call-update) | async-done | bytes 6291472 | tf_op jit(solution)/shard_map/all_gather | solution.py:268
  111.9 1.9 copy-done.6
  113.8 7.2 %shard_map.73 = bf16[512,256]{1,0:T(8,128)(2,1)S(1)} custom-call(bf16[512,6144]{1,0:T(8,128)(2,1)} %all-gather.2.cloned.1.call-done.rows_ref, bf16[6144,256]{1,0:T(8,128)(2,1)S(1)} %bitcast.57, bf16[6144,256]{1,0:T(8,128)(2,1)S(1)} %bitcast.55), custom_call_target="tpu_custom_call" | custom-call | flops 3221225472 | bytes 12582912 | tf_op jit(solution)/shard_map/pallas_call | solution.py:152
  121.2 18.0 %all_to_all.40.rows_ref = bf16[4,512,256]{2,1,0:T(8,128)(2,1)S(1)} all-to-all(bf16[4,512,256]{2,1,0:T(8,128)(2,1)S(1)} %broadcast_in_dim.24), channel_id=1, replica_groups={{0,8,16,24},{1,9,17,25},{2,10,18,26},{3,11,19,27},{4,12,20,28},{5,13,21..., dimensions={0} | all-to-all | bytes 2097152 | tf_op jit(solution)/shard_map/all_to_all | solution.py:52
  139.1 5.0 %shard_map.74 = bf16[512,1536]{1,0:T(8,128)(2,1)} custom-call(bf16[4,512,256]{2,1,0:T(8,128)(2,1)S(1)} %all_to_all.40.rows_ref, bf16[4,256,1536]{2,1,0:T(8,128)(2,1)} %all-to-all-done.1.down_ref), custom_call_target="tpu_custom_call" | custom-call | flops 1610612736 | bytes 5767168 | tf_op jit(solution)/shard_map/pallas_call | solution.py:207
  144.1 39.5 %all_to_all.41.up_ref = bf16[4,1536,256]{2,1,0:T(8,128)(2,1)S(1)} all-to-all(bf16[4,1536,256]{2,1,0:T(8,128)(2,1)} %bitcast.54), channel_id=1, replica_groups={{0,8,16,24},{1,9,17,25},{2,10,18,26},{3,11,19,27},{4,12,20,28},{5,13,21..., dimensions={0} | all-to-all | bytes 6291456 | tf_op jit(solution)/shard_map/all_to_all | solution.py:52
  183.7 1.7 reshape.91
  185.4 7.8 %all-to-all-start.4 = ((bf16[32,2,1536]{2,1,0:T(2,128)(2,1)}), bf16[32,2,1536]{2,1,0:T(2,128)(2,1)S(1)}, u32[]{:S(2)}, u32[]{:S(2)}) async-start(bf16[32,2,1536]{2,1,0:T(2,128)(2,1)} %reshape.91), calls=%async_computation.5 | async-start | bytes 393216 | tf_op jit(solution)/shard_map/all_to_all | solution.py:52
  193.3 8.0 %all-to-all-done.4 = bf16[32,2,1536]{2,1,0:T(2,128)(2,1)S(1)} async-done(((bf16[32,2,1536]{2,1,0:T(2,128)(2,1)}), bf16[32,2,1536]{2,1,0:T(2,128)(2,1)S(1)}, u32[]{:S(2)}, u32[]{:S(2)}) %all-to-all-start.4) | async-done | bytes 196640 | tf_op jit(solution)/shard_map/all_to_all | solution.py:52
  203.8 12.1 %all_to_all.42 = bf16[32,2,1536]{2,1,0:T(2,128)(2,1)S(1)} all-to-all(bf16[32,2,1536]{2,1,0:T(2,128)(2,1)S(1)} %bitcast.62), channel_id=1, replica_groups={{0,8,16,24,32,40,48,56,64,72,80,88,96,104,112,120,128,136,144,152,160,1..., dimensions={0} | all-to-all | bytes 393216 | tf_op jit(solution)/shard_map/all_to_all | solution.py:52
  216.1 2.7 collective-permute-start.5
  218.7 4.6 %collective-permute-done.2 = bf16[64,1536]{1,0:T(8,128)(2,1)} collective-permute-done((bf16[64,1536]{1,0:T(8,128)(2,1)S(1)}, bf16[64,1536]{1,0:T(8,128)(2,1)}, u32[]{:S(2)}, u32[]{:S(2)}) %collective-permute-start.2) | collective-permute-done | bytes 196640 | tf_op jit(solution)/shard_map/ppermute | solution.py:67
  223.3 2.7 collective-permute-start.6
  226.0 3.9 %collective-permute-done.3 = bf16[64,1536]{1,0:T(8,128)(2,1)} collective-permute-done((bf16[64,1536]{1,0:T(8,128)(2,1)}, bf16[64,1536]{1,0:T(8,128)(2,1)}, u32[]{:S(2)}, u32[]{:S(2)}) %collective-permute-start.3) | collective-permute-done | bytes 196640 | tf_op jit(solution)/shard_map/ppermute | solution.py:67
  229.8 2.4 constant_dynamic-slice_fusion
  232.2 2.7 collective-permute-start.7
  237.8 2.9 collective-permute-start.9
  240.8 1.5 collective-permute-done.9
  242.4 8.1 %collective-permute-done.10.gate_ref = bf16[1536,256]{1,0:T(8,128)(2,1)S(1)} collective-permute-done((bf16[1536,256]{1,0:T(8,128)(2,1)S(1)}, bf16[1536,256]{1,0:T(8,128)(2,1)S(1)}, u32[]{:S(2)}, u32[]{:S(2)}) %collective-permute-start.10) | collective-permute-done | bytes 786464 | tf_op jit(solution)/shard_map/ppermute | solution.py:67
  253.5 2.4 collective-permute-start.11
  255.9 1.4 copy-done.2
  262.9 1.8 collective-permute-done.13
  265.6 1.5 collective-permute-start.14
  267.1 1.4 copy-done.4
  270.6 2.9 collective-permute-done.12
  273.5 1.9 collective-permute-done.14
  275.4 1.4 convert_add_fusion
  277.1 12.8 %all_to_all.43.rows_ref = bf16[4,512,256]{2,1,0:T(8,128)(2,1)S(1)} all-to-all(bf16[4,512,256]{2,1,0:T(8,128)(2,1)S(1)} %broadcast_in_dim.25), channel_id=1, replica_groups={{0,8,16,24},{1,9,17,25},{2,10,18,26},{3,11,19,27},{4,12,20,28},{5,13,21..., dimensions={0} | all-to-all | bytes 2097152 | tf_op jit(solution)/shard_map/all_to_all | solution.py:52
  289.9 3.9 %shard_map.79 = bf16[512,1536]{1,0:T(8,128)(2,1)S(1)} custom-call(bf16[4,512,256]{2,1,0:T(8,128)(2,1)S(1)} %all_to_all.43.rows_ref, bf16[4,256,1536]{2,1,0:T(8,128)(2,1)} %all-to-all-done.1.down_ref), custom_call_target="tpu_custom_call" | custom-call | flops 1610612736 | bytes 5767168 | tf_op jit(solution)/shard_map/pallas_call | solution.py:207
  294.0 2.7 collective-permute-start.19
  296.6 2.0 collective-permute-done.15
  299.2 2.4 collective-permute-start.20
  301.6 2.9 collective-permute-done.16
  304.7 5.7 %collective-permute-done.17 = bf16[64,1536]{1,0:T(8,128)(2,1)S(1)} collective-permute-done((bf16[64,1536]{1,0:T(8,128)(2,1)S(1)}, bf16[64,1536]{1,0:T(8,128)(2,1)S(1)}, u32[]{:S(2)}, u32[]{:S(2)}) %collective-permute-start.17) | collective-permute-done | bytes 196640 | tf_op jit(solution)/shard_map/ppermute | solution.py:67
  312.0 3.2 collective-permute-done.21
  315.3 3.2 collective-permute-start.22
  318.5 2.6 collective-permute-done.22
  321.3 23.3 %all_to_all.44 = bf16[32,2,1536]{2,1,0:T(2,128)(2,1)S(1)} all-to-all(bf16[32,2,1536]{2,1,0:T(2,128)(2,1)S(1)} %reshape.100), channel_id=1, replica_groups={{0,8,16,24,32,40,48,56,64,72,80,88,96,104,112,120,128,136,144,152,160,1..., dimensions={0} | all-to-all | bytes 393216 | tf_op jit(solution)/shard_map/all_to_all | solution.py:52
  (118 shorter events, 29.0 us)
Async XLA Ops:
  6.5 0.7 copy-start
  12.3 22.2 %all-to-all-start = ((bf16[32,2,6144]{2,1,0:T(2,128)(2,1)}), bf16[32,2,6144]{2,1,0:T(2,128)(2,1)}, u32[]{:S(2)}, u32[]{:S(2)}) async-start(bf16[32,2,6144]{2,1,0:T(2,128)(2,1)} %bitcast.1), calls=%async_computation | async-start | bytes 1572864 | tf_op jit(solution)/shard_map/all_to_all | solution.py:52
  20.9 91.0 %all-gather.2.cloned.1.call-start = ((), (), s32[]{:S(2)}) async-start(), calls=%async_computation.9 | async-start | bytes 7077888 | tf_op jit(solution)/shard_map/all_gather | solution.py:268
  40.3 59.6 %all-to-all-start.1 = ((bf16[4,256,1536]{2,1,0:T(8,128)(2,1)}), bf16[4,256,1536]{2,1,0:T(8,128)(2,1)}, u32[]{:S(2)}, u32[]{:S(2)}) async-start(bf16[4,256,1536]{2,1,0:T(8,128)(2,1)} %bitcast.6), calls=%async_computation.1 | async-start | bytes 6291456 | tf_op jit(solution)/shard_map/all_to_all | solution.py:52
  45.0 138.7 %reduce-scatter.2.cloned.1.call-start = ((), (), s32[]{:S(2)}) async-start(), calls=%async_computation.10 | async-start | bytes 1769472 | tf_op jit(solution)/shard_map/reduce_scatter | solution.py:276
  45.1 66.9 %copy-start.5 = (bf16[1,6144,256]{2,1,0:T(8,128)(2,1)S(1)}, bf16[1,6144,256]{2,1,0:T(8,128)(2,1)}, u32[]{:S(2)}) copy-start(bf16[1,6144,256]{2,1,0:T(8,128)(2,1)} %param.10) | copy-start | bytes 9437188
  46.7 51.4 %collective-permute-start = (bf16[1536,256]{1,0:T(8,128)(2,1)S(1)}, bf16[1536,256]{1,0:T(8,128)(2,1)S(1)}, u32[]{:S(2)}, u32[]{:S(2)}) collective-permute-start(bf16[1536,256]{1,0:T(8,128)(2,1)S(1)} %get-tuple-element.44), channel_id=1, source_target_pairs={{0,8},{1,9},{2,10},{3,11},{4,12},{5,13},{6,14},{7,15},{8,16},{9,17... | collective-permute-start | bytes 2359304 | tf_op jit(solution)/shard_map/ppermute | solution.py:67
  48.1 50.9 %collective-permute-start.1 = (bf16[1536,256]{1,0:T(8,128)(2,1)S(1)}, bf16[1536,256]{1,0:T(8,128)(2,1)S(1)}, u32[]{:S(2)}, u32[]{:S(2)}) collective-permute-start(bf16[1536,256]{1,0:T(8,128)(2,1)S(1)} %get-tuple-element.43), channel_id=1, source_target_pairs={{0,24},{1,25},{2,26},{3,27},{4,28},{5,29},{6,30},{7,31},{8,0},{9,1... | collective-permute-start | bytes 2359304 | tf_op jit(solution)/shard_map/ppermute | solution.py:67
  98.1 0.9 copy-start.8
  99.0 0.9 copy-start.10
  111.9 1.9 copy-start.6
  144.1 57.3 %copy-start.12 = (bf16[4,6144]{1,0:T(4,128)(2,1)S(1)}, bf16[4,6144]{1,0:T(4,128)(2,1)}, u32[]{:S(2)}) copy-start(bf16[4,6144]{1,0:T(4,128)(2,1)} %param.7) | copy-start | bytes 147460
  185.4 16.0 %all-to-all-start.4 = ((bf16[32,2,1536]{2,1,0:T(2,128)(2,1)}), bf16[32,2,1536]{2,1,0:T(2,128)(2,1)S(1)}, u32[]{:S(2)}, u32[]{:S(2)}) async-start(bf16[32,2,1536]{2,1,0:T(2,128)(2,1)} %reshape.91), calls=%async_computation.5 | async-start | bytes 393216 | tf_op jit(solution)/shard_map/all_to_all | solution.py:52
  201.9 0.6 copy-start.14
  216.0 7.3 %collective-permute-start.2 = (bf16[64,1536]{1,0:T(8,128)(2,1)S(1)}, bf16[64,1536]{1,0:T(8,128)(2,1)}, u32[]{:S(2)}, u32[]{:S(2)}) collective-permute-start(bf16[64,1536]{1,0:T(8,128)(2,1)S(1)} %reshape.96), channel_id=1, source_target_pairs={{0,1},{1,2},{2,3},{3,4},{4,5},{5,6},{6,7},{7,0},{8,9},{9,10},{10,1... | collective-permute-start | bytes 589832 | tf_op jit(solution)/shard_map/ppermute | solution.py:67
  216.1 7.2 %collective-permute-start.5 = (bf16[64,1536]{1,0:T(8,128)(2,1)S(1)}, bf16[64,1536]{1,0:T(8,128)(2,1)S(1)}, u32[]{:S(2)}, u32[]{:S(2)}) collective-permute-start(bf16[64,1536]{1,0:T(8,128)(2,1)S(1)} %reshape.96), channel_id=1, source_target_pairs={{0,7},{1,0},{2,1},{3,2},{4,3},{5,4},{6,5},{7,6},{8,15},{9,8},{10,9... | collective-permute-start | bytes 589832 | tf_op jit(solution)/shard_map/ppermute | solution.py:67
  223.3 6.5 %collective-permute-start.3 = (bf16[64,1536]{1,0:T(8,128)(2,1)}, bf16[64,1536]{1,0:T(8,128)(2,1)}, u32[]{:S(2)}, u32[]{:S(2)}) collective-permute-start(bf16[64,1536]{1,0:T(8,128)(2,1)} %collective-permute-done.2), channel_id=1, source_target_pairs={{0,1},{1,2},{2,3},{3,4},{4,5},{5,6},{6,7},{7,0},{8,9},{9,10},{10,1... | collective-permute-start | bytes 589832 | tf_op jit(solution)/shard_map/ppermute | solution.py:67
  223.3 8.9 %collective-permute-start.6 = (bf16[64,1536]{1,0:T(8,128)(2,1)S(1)}, bf16[64,1536]{1,0:T(8,128)(2,1)S(1)}, u32[]{:S(2)}, u32[]{:S(2)}) collective-permute-start(bf16[64,1536]{1,0:T(8,128)(2,1)S(1)} %collective-permute-done.5), channel_id=1, source_target_pairs={{0,7},{1,0},{2,1},{3,2},{4,3},{5,4},{6,5},{7,6},{8,15},{9,8},{10,9... | collective-permute-start | bytes 589832 | tf_op jit(solution)/shard_map/ppermute | solution.py:67
  229.8 5.9 %collective-permute-start.4 = (bf16[64,1536]{1,0:T(8,128)(2,1)}, bf16[64,1536]{1,0:T(8,128)(2,1)S(1)}, u32[]{:S(2)}, u32[]{:S(2)}) collective-permute-start(bf16[64,1536]{1,0:T(8,128)(2,1)} %collective-permute-done.3), channel_id=1, source_target_pairs={{0,1},{1,2},{2,3},{3,4},{4,5},{5,6},{6,7},{7,0},{8,9},{9,10},{10,1... | collective-permute-start | bytes 589832 | tf_op jit(solution)/shard_map/ppermute | solution.py:67
  232.2 18.2 %collective-permute-start.10 = (bf16[1536,256]{1,0:T(8,128)(2,1)S(1)}, bf16[1536,256]{1,0:T(8,128)(2,1)S(1)}, u32[]{:S(2)}, u32[]{:S(2)}) collective-permute-start(bf16[1536,256]{1,0:T(8,128)(2,1)S(1)} %get-tuple-element.41), channel_id=1, source_target_pairs={{0,16},{1,17},{2,18},{3,19},{4,20},{5,21},{6,22},{7,23},{8,24},{9,... | collective-permute-start | bytes 2359304 | tf_op jit(solution)/shard_map/ppermute | solution.py:67
  232.2 5.6 %collective-permute-start.7 = (bf16[64,1536]{1,0:T(8,128)(2,1)S(1)}, bf16[64,1536]{1,0:T(8,128)(2,1)S(1)}, u32[]{:S(2)}, u32[]{:S(2)}) collective-permute-start(bf16[64,1536]{1,0:T(8,128)(2,1)S(1)} %collective-permute-done.6), channel_id=1, source_target_pairs={{0,7},{1,0},{2,1},{3,2},{4,3},{5,4},{6,5},{7,6},{8,15},{9,8},{10,9... | collective-permute-start | bytes 589832 | tf_op jit(solution)/shard_map/ppermute | solution.py:67
  235.8 5.1 %collective-permute-start.8 = (bf16[32,1536]{1,0:T(8,128)(2,1)S(1)}, bf16[32,1536]{1,0:T(8,128)(2,1)S(1)}, u32[]{:S(2)}, u32[]{:S(2)}) collective-permute-start(bf16[32,1536]{1,0:T(8,128)(2,1)S(1)} %slice.113), channel_id=1, source_target_pairs={{0,1},{1,2},{2,3},{3,4},{4,5},{5,6},{6,7},{7,0},{8,9},{9,10},{10,1... | collective-permute-start | bytes 294920 | tf_op jit(solution)/shard_map/ppermute | solution.py:67
  237.8 4.5 %collective-permute-start.9 = (bf16[32,1536]{1,0:T(8,128)(2,1)S(1)}, bf16[32,1536]{1,0:T(8,128)(2,1)S(1)}, u32[]{:S(2)}, u32[]{:S(2)}) collective-permute-start(bf16[32,1536]{1,0:T(8,128)(2,1)S(1)} %slice.114), channel_id=1, source_target_pairs={{0,7},{1,0},{2,1},{3,2},{4,3},{5,4},{6,5},{7,6},{8,15},{9,8},{10,9... | collective-permute-start | bytes 294920 | tf_op jit(solution)/shard_map/ppermute | solution.py:67
  251.4 1.2 copy-start.1
  253.5 7.6 %collective-permute-start.11 = (bf16[256,512]{1,0:T(8,128)(2,1)}, bf16[256,512]{1,0:T(8,128)(2,1)S(1)}, u32[]{:S(2)}, u32[]{:S(2)}) collective-permute-start(bf16[256,512]{1,0:T(8,128)(2,1)} %get-tuple-element.53), channel_id=1, source_target_pairs={{0,8},{1,9},{2,10},{3,11},{4,12},{5,13},{6,14},{7,15},{8,16},{9,17... | collective-permute-start | bytes 786440 | tf_op jit(solution)/shard_map/ppermute | solution.py:67
  255.9 1.4 copy-start.2
  257.3 1.1 copy-start.11
  258.4 1.0 copy-start.16
  258.4 1.5 copy-start.3
  258.4 1.7 copy-start.9
  259.4 5.3 %collective-permute-start.13 = (bf16[256,512]{1,0:T(8,128)(2,1)S(1)}, bf16[256,512]{1,0:T(8,128)(2,1)S(1)}, u32[]{:S(2)}, u32[]{:S(2)}) collective-permute-start(bf16[256,512]{1,0:T(8,128)(2,1)S(1)} %copy-done.16), channel_id=1, source_target_pairs={{0,24},{1,25},{2,26},{3,27},{4,28},{5,29},{6,30},{7,31},{8,0},{9,1... | collective-permute-start | bytes 786440 | tf_op jit(solution)/shard_map/ppermute | solution.py:67
  262.0 11.5 %collective-permute-start.12 = (bf16[512,512]{1,0:T(8,128)(2,1)}, bf16[512,512]{1,0:T(8,128)(2,1)}, u32[]{:S(2)}, u32[]{:S(2)}) collective-permute-start(bf16[512,512]{1,0:T(8,128)(2,1)} %pad_maximum_fusion), channel_id=1, source_target_pairs={{0,8},{1,9},{2,10},{3,11},{4,12},{5,13},{6,14},{7,15},{8,16},{9,17... | collective-permute-start | bytes 1572872 | tf_op jit(solution)/shard_map/ppermute | solution.py:67
  265.6 9.8 %collective-permute-start.14 = (bf16[512,512]{1,0:T(8,128)(2,1)}, bf16[512,512]{1,0:T(8,128)(2,1)}, u32[]{:S(2)}, u32[]{:S(2)}) collective-permute-start(bf16[512,512]{1,0:T(8,128)(2,1)} %pad_maximum_fusion.1), channel_id=1, source_target_pairs={{0,24},{1,25},{2,26},{3,27},{4,28},{5,29},{6,30},{7,31},{8,0},{9,1... | collective-permute-start | bytes 1572872 | tf_op jit(solution)/shard_map/ppermute | solution.py:67
  267.1 1.4 copy-start.4
  268.5 1.1 copy-start.7
  293.9 4.8 %collective-permute-start.15 = (bf16[32,1536]{1,0:T(8,128)(2,1)S(1)}, bf16[32,1536]{1,0:T(8,128)(2,1)S(1)}, u32[]{:S(2)}, u32[]{:S(2)}) collective-permute-start(bf16[32,1536]{1,0:T(8,128)(2,1)S(1)} %get-tuple-element.49), channel_id=1, source_target_pairs={{0,1},{1,2},{2,3},{3,4},{4,5},{5,6},{6,7},{7,0},{8,9},{9,10},{10,1... | collective-permute-start | bytes 294920 | tf_op jit(solution)/shard_map/ppermute | solution.py:67
  294.0 4.7 %collective-permute-start.19 = (bf16[32,1536]{1,0:T(8,128)(2,1)S(1)}, bf16[32,1536]{1,0:T(8,128)(2,1)S(1)}, u32[]{:S(2)}, u32[]{:S(2)}) collective-permute-start(bf16[32,1536]{1,0:T(8,128)(2,1)S(1)} %get-tuple-element.50), channel_id=1, source_target_pairs={{0,7},{1,0},{2,1},{3,2},{4,3},{5,4},{6,5},{7,6},{8,15},{9,8},{10,9... | collective-permute-start | bytes 294920 | tf_op jit(solution)/shard_map/ppermute | solution.py:67
  298.7 5.8 %collective-permute-start.16 = (bf16[64,1536]{1,0:T(8,128)(2,1)S(1)}, bf16[64,1536]{1,0:T(8,128)(2,1)S(1)}, u32[]{:S(2)}, u32[]{:S(2)}) collective-permute-start(bf16[64,1536]{1,0:T(8,128)(2,1)S(1)} %pad_maximum_fusion.2), channel_id=1, source_target_pairs={{0,1},{1,2},{2,3},{3,4},{4,5},{5,6},{6,7},{7,0},{8,9},{9,10},{10,1... | collective-permute-start | bytes 589832 | tf_op jit(solution)/shard_map/ppermute | solution.py:67
  299.2 5.5 %collective-permute-start.20 = (bf16[64,1536]{1,0:T(8,128)(2,1)S(1)}, bf16[64,1536]{1,0:T(8,128)(2,1)S(1)}, u32[]{:S(2)}, u32[]{:S(2)}) collective-permute-start(bf16[64,1536]{1,0:T(8,128)(2,1)S(1)} %pad_maximum_fusion.3), channel_id=1, source_target_pairs={{0,7},{1,0},{2,1},{3,2},{4,3},{5,4},{6,5},{7,6},{8,15},{9,8},{10,9... | collective-permute-start | bytes 589832 | tf_op jit(solution)/shard_map/ppermute | solution.py:67
  304.6 5.8 %collective-permute-start.17 = (bf16[64,1536]{1,0:T(8,128)(2,1)S(1)}, bf16[64,1536]{1,0:T(8,128)(2,1)S(1)}, u32[]{:S(2)}, u32[]{:S(2)}) collective-permute-start(bf16[64,1536]{1,0:T(8,128)(2,1)S(1)} %add_convert_fusion.6), channel_id=1, source_target_pairs={{0,1},{1,2},{2,3},{3,4},{4,5},{5,6},{6,7},{7,0},{8,9},{9,10},{10,1... | collective-permute-start | bytes 589832 | tf_op jit(solution)/shard_map/ppermute | solution.py:67
  310.5 34.2 %copy-start.13 = (bf16[4,6144]{1,0:T(4,128)(2,1)S(1)}, bf16[4,6144]{1,0:T(4,128)(2,1)}, u32[]{:S(2)}) copy-start(bf16[4,6144]{1,0:T(4,128)(2,1)} %param.7) | copy-start | bytes 147460
  310.5 34.2 %copy-start.15 = (f32[4,6144]{1,0:T(4,128)S(1)}, f32[4,6144]{1,0:T(4,128)}, u32[]{:S(2)}) copy-start(f32[4,6144]{1,0:T(4,128)} %copy-done.14) | copy-start | bytes 294916
  310.5 4.7 %collective-permute-start.21 = (bf16[64,1536]{1,0:T(8,128)(2,1)S(1)}, bf16[64,1536]{1,0:T(8,128)(2,1)S(1)}, u32[]{:S(2)}, u32[]{:S(2)}) collective-permute-start(bf16[64,1536]{1,0:T(8,128)(2,1)S(1)} %get-tuple-element.46), channel_id=1, source_target_pairs={{0,7},{1,0},{2,1},{3,2},{4,3},{5,4},{6,5},{7,6},{8,15},{9,8},{10,9... | collective-permute-start | bytes 589832 | tf_op jit(solution)/shard_map/ppermute | solution.py:67
  310.8 7.7 %collective-permute-start.18 = (bf16[64,1536]{1,0:T(8,128)(2,1)S(1)}, bf16[64,1536]{1,0:T(8,128)(2,1)S(1)}, u32[]{:S(2)}, u32[]{:S(2)}) collective-permute-start(bf16[64,1536]{1,0:T(8,128)(2,1)S(1)} %get-tuple-element.45), channel_id=1, source_target_pairs={{0,1},{1,2},{2,3},{3,4},{4,5},{5,6},{6,7},{7,0},{8,9},{9,10},{10,1... | collective-permute-start | bytes 589832 | tf_op jit(solution)/shard_map/ppermute | solution.py:67
  315.3 5.8 %collective-permute-start.22 = (bf16[64,1536]{1,0:T(8,128)(2,1)S(1)}, bf16[64,1536]{1,0:T(8,128)(2,1)S(1)}, u32[]{:S(2)}, u32[]{:S(2)}) collective-permute-start(bf16[64,1536]{1,0:T(8,128)(2,1)S(1)} %add_convert_fusion.3), channel_id=1, source_target_pairs={{0,7},{1,0},{2,1},{3,2},{4,3},{5,4},{6,5},{7,6},{8,15},{9,8},{10,9... | collective-permute-start | bytes 589832 | tf_op jit(solution)/shard_map/ppermute | solution.py:67
Sparse Core Ops, SparseCore 0:
  37.6 74.2 all-gather.1
  144.3 34.3 reduce-scatter.1

commit v2 on v1

--- a/solution.py
+++ b/solution.py
@@ -97,11 +97,12 @@
     return wide[0] + up + down
 
 
-def feature_part(weight, position, hidden, step):
+def feature_part(weight, position, hidden, step, first=0, last=1, of=1):
     depth = hidden // RING
     part = weight.shape[0] // RING
-    start = lax.rem(position // depth + step, RING) * part
-    rows = lax.dynamic_slice_in_dim(weight, start, part, 0)
+    piece = part // of
+    start = lax.rem(position // depth + step, RING) * part + first * piece
+    rows = lax.dynamic_slice_in_dim(weight, start, (last - first) * piece, 0)
     return shift(rows, hidden, step, "across") if step else rows
 
 
@@ -126,47 +127,82 @@
 def whole_gate_up(rows, gate, up):
     count, width = rows.shape
     units = gate.shape[1]
-    depth = width // 6
-
-    def kernel(rows_ref, gate_ref, up_ref, out_ref, gate_sum, up_sum):
-        step = pl.program_id(0)
-        block = rows_ref[...]
-        features = pl.ds(pl.multiple_of(step * depth, depth), depth)
-        gate_part = jnp.dot(block, gate_ref[features, :], preferred_element_type=F32)
-        up_part = jnp.dot(block, up_ref[features, :], preferred_element_type=F32)
-
-        @pl.when(step == 0)
-        def _():
-            gate_sum[...] = gate_part
-            up_sum[...] = up_part
-
-        @pl.when(step > 0)
-        def _():
-            gate_sum[...] += gate_part
-            up_sum[...] += up_part
-
-        @pl.when(step == pl.num_programs(0) - 1)
-        def _():
-            out_ref[...] = silu_product(gate_sum[...], up_sum[...])
-
+    pieces = 6
+    depth = width // pieces
+
+    def kernel(rows_hbm, gate_hbm, up_hbm, out_ref, rows_ref, gate_ref, up_ref, sems):
+        copies = []
+        for piece in range(pieces):
+            features = pl.ds(piece * depth, depth)
+            moved = [
+                pltpu.make_async_copy(
+                    rows_hbm.at[:, features], rows_ref.at[piece], sems.at[piece, 0]
+                ),
+                pltpu.make_async_copy(gate_hbm.at[features], gate_ref.at[piece], sems.at[piece, 1]),
+                pltpu.make_async_copy(up_hbm.at[features], up_ref.at[piece], sems.at[piece, 2]),
+            ]
+            for copy in moved:
+                copy.start()
+            copies.append(moved)
+        for copy in copies[0]:
+            copy.wait()
+        gate_sum = jnp.dot(rows_ref[0], gate_ref[0], preferred_element_type=F32)
+        up_sum = jnp.dot(rows_ref[0], up_ref[0], preferred_element_type=F32)
+        for piece in range(1, pieces):
+            for copy in copies[piece]:
+                copy.wait()
+            gate_sum += jnp.dot(rows_ref[piece], gate_ref[piece], preferred_element_type=F32)
+            up_sum += jnp.dot(rows_ref[piece], up_ref[piece], preferred_element_type=F32)
+        out_ref[...] = silu_product(gate_sum, up_sum)
+
+    anywhere = pl.BlockSpec(memory_space=pl.ANY)
     return pl.pallas_call(
         kernel,
-        grid=(width // depth,),
-        in_specs=[
-            pl.BlockSpec((count, depth), lambda k: (0, k)),
-            whole_block(),
-            whole_block(),
+        in_specs=[anywhere, anywhere, anywhere],
+        out_specs=whole_block(),
+        out_shape=jax.ShapeDtypeStruct((count, units), BF16),
+        scratch_shapes=[
+            pltpu.VMEM((pieces, count, depth), BF16),
+            pltpu.VMEM((pieces, depth, units), BF16),
+            pltpu.VMEM((pieces, depth, units), BF16),
+            pltpu.SemaphoreType.DMA((pieces, 3)),
         ],
-        out_specs=pl.BlockSpec((count, units), lambda k: (0, 0)),
-        out_shape=jax.ShapeDtypeStruct((count, units), BF16),
-        scratch_shapes=[pltpu.VMEM((count, units), F32), pltpu.VMEM((count, units), F32)],
-        compiler_params=params(24),
+        compiler_params=pltpu.CompilerParams(vmem_limit_bytes=32 * 1024 * 1024),
         cost_estimate=pl.CostEstimate(
             flops=4 * count * width * units,
             bytes_accessed=2 * (count * width + 2 * width * units),
             transcendentals=count * units,
         ),
-    )(hold(rows), gate, up)
+    )(hold(rows), hold(gate), hold(up))
+
+
+def feature_blocks(weight):
+    units, width = weight.shape
+    part = width // RING
+
+    def kernel(weight_hbm, out_ref, sems):
+        moved = [
+            pltpu.make_async_copy(
+                weight_hbm.at[:, pl.ds(y * part, part)], out_ref.at[y], sems.at[y]
+            )
+            for y in range(RING)
+        ]
+        for copy in moved:
+            copy.start()
+        for copy in moved:
+            copy.wait()
+
+    return pl.pallas_call(
+        kernel,
+        in_specs=[pl.BlockSpec(memory_space=pl.ANY)],
+        out_specs=whole_block(),
+        out_shape=jax.ShapeDtypeStruct((RING, units, part), BF16),
+        scratch_shapes=[pltpu.SemaphoreType.DMA((RING,))],
+        compiler_params=pltpu.CompilerParams(vmem_limit_bytes=4 * 1024 * 1024),
+        cost_estimate=pl.CostEstimate(
+            flops=0, bytes_accessed=4 * units * width, transcendentals=0
+        ),
+    )(hold(weight))
 
 
 def part_gate_up(rows, gate, up_parts, place):
@@ -264,11 +300,9 @@
     rows = rows.reshape(block, width)
     gate, up, down = gate_weight[0], up_weight[0], down_weight[0]
     near = [feature_part(gate, position, hidden, step) for step in (1, 3)]
-    rows, down_in = lax.optimization_barrier((rows, down))
+    near.append(feature_part(gate, position, hidden, 2, 0, 1, 2))
     gathered = lax.all_gather(rows, "hidden", axis=0, tiled=True, axis_index_groups=along)
-    down_parts = exchange(
-        down_in.reshape(units, RING, part).transpose(1, 0, 2), "hidden", across
-    )
+    down_parts = exchange(feature_blocks(down), "hidden", across)
     gathered, near, down_parts = lax.optimization_barrier((gathered, near, down_parts))
     partial = finish(whole_gate_up(gathered, gate, up), down_parts)
     partial, up_in = lax.optimization_barrier((partial, up))
@@ -283,12 +317,13 @@
     rows = outgoing(state).reshape(experts, capacity, RING, part).transpose(0, 2, 1, 3)
     rows = exchange(rows.reshape(experts * RING, capacity, part), both, homes)
     rows, gate_in = lax.optimization_barrier((rows, gate))
-    far = [feature_part(gate_in, position, hidden, step) for step in (0, 2)]
-    gate_parts = [far[0], near[0], far[1], near[1]]
+    far = feature_part(gate_in, position, hidden, 2, 1, 2, 2)
     blocks = ring_gather(rows.reshape(block, part), hidden)
     offsets = sorted(blocks)
     gathered = jnp.concatenate([blocks[step] for step in offsets])
-    gathered, gate_parts = lax.optimization_barrier((gathered, gate_parts))
+    gathered, far = lax.optimization_barrier((gathered, far))
+    own = feature_part(gate, position, hidden, 0)
+    gate_parts = [own, near[0], jnp.concatenate([near[2], far]), near[1]]
     values = {
         step: part_gate_up(
             gathered,

time: 354 us -> 337 us (0.952)
  waiting for transfers between devices: 121 us -> 96.5 us
  blocking collectives: 106 us -> 129 us
  local copies, waits for them, and re-layouts: 32.7 us -> 21.9 us
  starting transfers between devices: 50.5 us -> 45.2 us
    all_to_all x5 -> x6, blocking collectives: 106 us -> 129 us  [exchange(): lax.all_to_all(values, axis, 0, 0, tiled=True, axis_index_groups=groups)]
    all_to_all x3 -> x2, waiting for transfers between devices: 18.4 us -> 8.01 us  [exchange(): lax.all_to_all(values, axis, 0, 0, tiled=True, axis_index_groups=groups)]
    all_to_all x3 -> x2, starting transfers between devices: 21.1 us -> 11.5 us  [exchange(): lax.all_to_all(values, axis, 0, 0, tiled=True, axis_index_groups=groups)]
    all_gather x1, waiting for transfers between devices: 12 us -> 4.55 us  [on_device(): lax.all_gather(rows, 'hidden', axis=0, tiled=True, axis_index_groups=along)]
    ppermute x23 -> x24, waiting for transfers between devices: 90.6 us -> 84 us  [shift(): return lax.ppermute(values, 'hidden', shifts(hidden, step, ring))]
    unnamed x44 -> x45, local copies, waits for them, and re-layouts: 16.8 us -> 10.3 us
    ppermute x23 -> x24, starting transfers between devices: 29.4 us -> 33.6 us  [shift(): return lax.ppermute(values, 'hidden', shifts(hidden, step, ring))]
    pallas_call x2, Pallas kernels: 8.89 us -> 4.88 us  [down_product(): pl.pallas_call(kernel, grid=(part // columns,), in_specs=[whole_block(),...]
  transfers between devices with their start and end apart: 28 -> 28, of which waited for: 18 -> 13; matrix products, arithmetic and copies ran while one was open for 4% -> 3% of each run, Pallas kernels for 1% -> 3%
where the time goes in v2:
time: 337 us; the launch traced here: 336 us
  blocking collectives  129 us (38%)
  waiting for transfers between devices  96.5 us (29%)
  starting transfers between devices  45.2 us (13%)
  local copies, waits for them, and re-layouts  21.9 us (6%)
  Pallas kernels  20.7 us (6%)
  between operations  14 us (4%)
  other arithmetic  5.04 us (1%)
  matrix products  3.46 us (1%)
    all_to_all x6, blocking collectives, exchange(): lax.all_to_all(values, axis, 0, 0, tiled=True, axis_index_groups=groups)  129 us
    ppermute x24, waiting for transfers between devices, shift(): return lax.ppermute(values, 'hidden', shifts(hidden, step, ring))  84 us
    ppermute x24, starting transfers between devices, shift(): return lax.ppermute(values, 'hidden', shifts(hidden, step, ring))  33.6 us
    all_to_all x2, starting transfers between devices, exchange(): lax.all_to_all(values, axis, 0, 0, tiled=True, axis_index_groups=groups)  11.5 us
    unnamed x45, local copies, waits for them, and re-layouts  10.3 us
    all_to_all x2, waiting for transfers between devices, exchange(): lax.all_to_all(values, axis, 0, 0, tiled=True, axis_index_groups=groups)  8.01 us
  transfers between devices with their start and end apart: 28, of which 13 were waited for; matrix products, arithmetic and copies ran while one was open for 3% of the time, Pallas kernels for 3%

profile of v2, /device:TPU:1, one launch (start us, length us, event | category | flops | bytes accessed | tf_op | source)
XLA Modules:
  0.0 336.1 jit_solution(2954240882968548730)
XLA Ops:
  11.3 21.9 %all_to_all.40 = bf16[32,2,6144]{2,1,0:T(2,128)(2,1)S(1)} all-to-all(bf16[32,2,6144]{2,1,0:T(2,128)(2,1)S(1)} %bitcast.61), channel_id=1, replica_groups={{0,8,16,24,32,40,48,56,64,72,80,88,96,104,112,120,128,136,144,152,160,1..., dimensions={0} | all-to-all | bytes 1572864 | tf_op jit(solution)/shard_map/all_to_all | solution.py:52
  33.3 1.2 reshape.87
  34.5 3.6 %shard_map.73 = bf16[4,256,1536]{2,1,0:T(8,128)(2,1)} custom-call(bf16[256,6144]{1,0:T(8,128)(2,1)} %bitcast.60), custom_call_target="tpu_custom_call" | custom-call | bytes 6291456 | tf_op jit(solution)/shard_map/pallas_call | solution.py:195
  38.1 3.7 %all-to-all-start.1 = ((bf16[4,256,1536]{2,1,0:T(8,128)(2,1)}), bf16[4,256,1536]{2,1,0:T(8,128)(2,1)S(1)}, u32[]{:S(2)}, u32[]{:S(2)}) async-start(bf16[4,256,1536]{2,1,0:T(8,128)(2,1)} %shard_map.73), calls=%async_computation.1 | async-start | bytes 6291456 | tf_op jit(solution)/shard_map/all_to_all | solution.py:52
  41.9 3.1 dynamic-slice_bitcast_fusion
  45.0 1.3 collective-permute-start
  46.3 1.4 collective-permute-start.1
  48.7 1.7 collective-permute-start.2
  50.4 53.2 %collective-permute-done.2 = bf16[768,256]{1,0:T(8,128)(2,1)S(1)} collective-permute-done((bf16[768,256]{1,0:T(8,128)(2,1)S(1)}, bf16[768,256]{1,0:T(8,128)(2,1)S(1)}, u32[]{:S(2)}, u32[]{:S(2)}) %collective-permute-start.2) | collective-permute-done | bytes 393248 | tf_op jit(solution)/shard_map/ppermute | solution.py:67
  104.4 4.5 %all-gather.2.cloned.1.call-done.rows_hbm = bf16[512,6144]{1,0:T(8,128)(2,1)} async-done(((bf16[64,6144]{1,0:T(8,128)(2,1)}), bf16[512,6144]{1,0:T(8,128)(2,1)}) %all-gather.2.cloned.1.call-update) | async-done | bytes 6291472 | tf_op jit(solution)/shard_map/all_gather | solution.py:304
  108.9 6.0 %shard_map.74 = bf16[512,256]{1,0:T(8,128)(2,1)S(1)} custom-call(bf16[512,6144]{1,0:T(8,128)(2,1)} %all-gather.2.cloned.1.call-done.rows_hbm, bf16[6144,256]{1,0:T(8,128)(2,1)} %bitcast.58, bf16[6144,256]{1,0:T(8,128)(2,1)} %bitcast.56), custom_call_target="tpu_custom_call" | custom-call | flops 3221225472 | bytes 12582912 | tf_op jit(solution)/shard_map/pallas_call | solution.py:159
  115.0 18.0 %all_to_all.41.rows_ref = bf16[4,512,256]{2,1,0:T(8,128)(2,1)S(1)} all-to-all(bf16[4,512,256]{2,1,0:T(8,128)(2,1)S(1)} %broadcast_in_dim.24), channel_id=1, replica_groups={{0,8,16,24},{1,9,17,25},{2,10,18,26},{3,11,19,27},{4,12,20,28},{5,13,21..., dimensions={0} | all-to-all | bytes 2097152 | tf_op jit(solution)/shard_map/all_to_all | solution.py:52
  133.0 2.4 shard_map.75
  135.4 1.2 copy-done.8
  136.7 39.5 %all_to_all.42.up_ref = bf16[4,1536,256]{2,1,0:T(8,128)(2,1)S(1)} all-to-all(bf16[4,1536,256]{2,1,0:T(8,128)(2,1)} %bitcast.57), channel_id=1, replica_groups={{0,8,16,24},{1,9,17,25},{2,10,18,26},{3,11,19,27},{4,12,20,28},{5,13,21..., dimensions={0} | all-to-all | bytes 6291456 | tf_op jit(solution)/shard_map/all_to_all | solution.py:52
  176.2 1.7 reshape.89
  177.9 7.8 %all-to-all-start.4 = ((bf16[32,2,1536]{2,1,0:T(2,128)(2,1)}), bf16[32,2,1536]{2,1,0:T(2,128)(2,1)S(1)}, u32[]{:S(2)}, u32[]{:S(2)}) async-start(bf16[32,2,1536]{2,1,0:T(2,128)(2,1)} %reshape.89), calls=%async_computation.5 | async-start | bytes 393216 | tf_op jit(solution)/shard_map/all_to_all | solution.py:52
  185.9 8.0 %all-to-all-done.4 = bf16[32,2,1536]{2,1,0:T(2,128)(2,1)S(1)} async-done(((bf16[32,2,1536]{2,1,0:T(2,128)(2,1)}), bf16[32,2,1536]{2,1,0:T(2,128)(2,1)S(1)}, u32[]{:S(2)}, u32[]{:S(2)}) %all-to-all-start.4) | async-done | bytes 196640 | tf_op jit(solution)/shard_map/all_to_all | solution.py:52
  196.4 12.1 %all_to_all.43 = bf16[32,2,1536]{2,1,0:T(2,128)(2,1)S(1)} all-to-all(bf16[32,2,1536]{2,1,0:T(2,128)(2,1)S(1)} %bitcast.65), channel_id=1, replica_groups={{0,8,16,24,32,40,48,56,64,72,80,88,96,104,112,120,128,136,144,152,160,1..., dimensions={0} | all-to-all | bytes 393216 | tf_op jit(solution)/shard_map/all_to_all | solution.py:52
  208.6 2.7 collective-permute-start.6
  211.3 4.5 %collective-permute-done.3 = bf16[64,1536]{1,0:T(8,128)(2,1)S(1)} collective-permute-done((bf16[64,1536]{1,0:T(8,128)(2,1)S(1)}, bf16[64,1536]{1,0:T(8,128)(2,1)S(1)}, u32[]{:S(2)}, u32[]{:S(2)}) %collective-permute-start.3) | collective-permute-done | bytes 196640 | tf_op jit(solution)/shard_map/ppermute | solution.py:67
  215.7 2.7 collective-permute-start.7
  218.4 3.6 %collective-permute-done.4 = bf16[64,1536]{1,0:T(8,128)(2,1)} collective-permute-done((bf16[64,1536]{1,0:T(8,128)(2,1)S(1)}, bf16[64,1536]{1,0:T(8,128)(2,1)}, u32[]{:S(2)}, u32[]{:S(2)}) %collective-permute-start.4) | collective-permute-done | bytes 196640 | tf_op jit(solution)/shard_map/ppermute | solution.py:67
  223.2 2.7 collective-permute-start.8
  226.0 2.0 collective-permute-done.5
  229.2 2.9 collective-permute-start.10
  236.0 1.7 collective-permute-start.12
  237.7 1.4 copy-done.2
  239.1 2.2 shard_map.77
  241.4 2.7 collective-permute-start.14
  244.1 2.1 shard_map.79
  248.3 3.1 collective-permute-start.15
  251.4 1.4 copy-done.4
  252.8 1.1 copy-done.7
  254.9 3.3 collective-permute-done.13
  258.2 1.4 convert_add_fusion
  259.9 14.5 %all_to_all.44.rows_ref = bf16[4,512,256]{2,1,0:T(8,128)(2,1)S(1)} all-to-all(bf16[4,512,256]{2,1,0:T(8,128)(2,1)S(1)} %broadcast_in_dim.25), channel_id=1, replica_groups={{0,8,16,24},{1,9,17,25},{2,10,18,26},{3,11,19,27},{4,12,20,28},{5,13,21..., dimensions={0} | all-to-all | bytes 2097152 | tf_op jit(solution)/shard_map/all_to_all | solution.py:52
  274.4 2.4 shard_map.80
  277.2 2.7 collective-permute-start.20
  279.9 2.0 collective-permute-done.16
  282.8 2.0 collective-permute-start.21
  284.8 2.9 collective-permute-done.17
  288.1 5.5 %collective-permute-done.18 = bf16[64,1536]{1,0:T(8,128)(2,1)S(1)} collective-permute-done((bf16[64,1536]{1,0:T(8,128)(2,1)S(1)}, bf16[64,1536]{1,0:T(8,128)(2,1)S(1)}, u32[]{:S(2)}, u32[]{:S(2)}) %collective-permute-start.18) | collective-permute-done | bytes 196640 | tf_op jit(solution)/shard_map/ppermute | solution.py:67
  294.1 1.2 collective-permute-start.19
  295.3 4.0 %collective-permute-done.22 = bf16[64,1536]{1,0:T(8,128)(2,1)S(1)} collective-permute-done((bf16[64,1536]{1,0:T(8,128)(2,1)S(1)}, bf16[64,1536]{1,0:T(8,128)(2,1)S(1)}, u32[]{:S(2)}, u32[]{:S(2)}) %collective-permute-start.22) | collective-permute-done | bytes 196640 | tf_op jit(solution)/shard_map/ppermute | solution.py:67
  299.3 2.9 collective-permute-start.23
  302.2 2.6 collective-permute-done.23
  305.0 23.2 %all_to_all.45 = bf16[32,2,1536]{2,1,0:T(2,128)(2,1)S(1)} all-to-all(bf16[32,2,1536]{2,1,0:T(2,128)(2,1)S(1)} %reshape.98), channel_id=1, replica_groups={{0,8,16,24,32,40,48,56,64,72,80,88,96,104,112,120,128,136,144,152,160,1..., dimensions={0} | all-to-all | bytes 393216 | tf_op jit(solution)/shard_map/all_to_all | solution.py:52
  (122 shorter events, 22.2 us)
Async XLA Ops:
  6.5 0.7 copy-start
  6.5 102.4 %all-gather.2.cloned.1.call-start = ((), (), s32[]{:S(2)}) async-start(), calls=%async_computation.9 | async-start | bytes 7077888 | tf_op jit(solution)/shard_map/all_gather | solution.py:304
  38.1 66.3 %all-to-all-start.1 = ((bf16[4,256,1536]{2,1,0:T(8,128)(2,1)}), bf16[4,256,1536]{2,1,0:T(8,128)(2,1)S(1)}, u32[]{:S(2)}, u32[]{:S(2)}) async-start(bf16[4,256,1536]{2,1,0:T(8,128)(2,1)} %shard_map.73), calls=%async_computation.1 | async-start | bytes 6291456 | tf_op jit(solution)/shard_map/all_to_all | solution.py:52
  41.8 134.4 %reduce-scatter.2.cloned.1.call-start = ((), (), s32[]{:S(2)}) async-start(), calls=%async_computation.10 | async-start | bytes 1769472 | tf_op jit(solution)/shard_map/reduce_scatter | solution.py:310
  45.0 58.6 %collective-permute-start = (bf16[1536,256]{1,0:T(8,128)(2,1)}, bf16[1536,256]{1,0:T(8,128)(2,1)}, u32[]{:S(2)}, u32[]{:S(2)}) collective-permute-start(bf16[1536,256]{1,0:T(8,128)(2,1)} %get-tuple-element.35), channel_id=1, source_target_pairs={{0,8},{1,9},{2,10},{3,11},{4,12},{5,13},{6,14},{7,15},{8,16},{9,17... | collective-permute-start | bytes 2359304 | tf_op jit(solution)/shard_map/ppermute | solution.py:67
  46.3 58.1 %collective-permute-start.1 = (bf16[1536,256]{1,0:T(8,128)(2,1)}, bf16[1536,256]{1,0:T(8,128)(2,1)}, u32[]{:S(2)}, u32[]{:S(2)}) collective-permute-start(bf16[1536,256]{1,0:T(8,128)(2,1)} %get-tuple-element.34), channel_id=1, source_target_pairs={{0,24},{1,25},{2,26},{3,27},{4,28},{5,29},{6,30},{7,31},{8,0},{9,1... | collective-permute-start | bytes 2359304 | tf_op jit(solution)/shard_map/ppermute | solution.py:67
  48.7 54.9 %collective-permute-start.2 = (bf16[768,256]{1,0:T(8,128)(2,1)S(1)}, bf16[768,256]{1,0:T(8,128)(2,1)S(1)}, u32[]{:S(2)}, u32[]{:S(2)}) collective-permute-start(bf16[768,256]{1,0:T(8,128)(2,1)S(1)} %dynamic-slice_bitcast_fusion.3), channel_id=1, source_target_pairs={{0,16},{1,17},{2,18},{3,19},{4,20},{5,21},{6,22},{7,23},{8,24},{9,... | collective-permute-start | bytes 1179656 | tf_op jit(solution)/shard_map/ppermute | solution.py:67
  103.6 0.8 copy-start.11
  104.4 28.6 %copy-start.5 = (bf16[4,256,1536]{2,1,0:T(8,128)(2,1)}, bf16[4,256,1536]{2,1,0:T(8,128)(2,1)S(1)}, u32[]{:S(2)}) copy-start(bf16[4,256,1536]{2,1,0:T(8,128)(2,1)S(1)} %all-to-all-done.1.down_ref) | copy-start | bytes 9437188
  135.4 1.2 copy-start.8
  136.6 57.3 %copy-start.9 = (bf16[4,6144]{1,0:T(4,128)(2,1)S(1)}, bf16[4,6144]{1,0:T(4,128)(2,1)}, u32[]{:S(2)}) copy-start(bf16[4,6144]{1,0:T(4,128)(2,1)} %param.7) | copy-start | bytes 147460
  177.9 16.0 %all-to-all-start.4 = ((bf16[32,2,1536]{2,1,0:T(2,128)(2,1)}), bf16[32,2,1536]{2,1,0:T(2,128)(2,1)S(1)}, u32[]{:S(2)}, u32[]{:S(2)}) async-start(bf16[32,2,1536]{2,1,0:T(2,128)(2,1)} %reshape.89), calls=%async_computation.5 | async-start | bytes 393216 | tf_op jit(solution)/shard_map/all_to_all | solution.py:52
  194.4 0.6 copy-start.13
  208.5 7.2 %collective-permute-start.3 = (bf16[64,1536]{1,0:T(8,128)(2,1)S(1)}, bf16[64,1536]{1,0:T(8,128)(2,1)S(1)}, u32[]{:S(2)}, u32[]{:S(2)}) collective-permute-start(bf16[64,1536]{1,0:T(8,128)(2,1)S(1)} %reshape.94), channel_id=1, source_target_pairs={{0,1},{1,2},{2,3},{3,4},{4,5},{5,6},{6,7},{7,0},{8,9},{9,10},{10,1... | collective-permute-start | bytes 589832 | tf_op jit(solution)/shard_map/ppermute | solution.py:67
  208.6 7.1 %collective-permute-start.6 = (bf16[64,1536]{1,0:T(8,128)(2,1)S(1)}, bf16[64,1536]{1,0:T(8,128)(2,1)}, u32[]{:S(2)}, u32[]{:S(2)}) collective-permute-start(bf16[64,1536]{1,0:T(8,128)(2,1)S(1)} %reshape.94), channel_id=1, source_target_pairs={{0,7},{1,0},{2,1},{3,2},{4,3},{5,4},{6,5},{7,6},{8,15},{9,8},{10,9... | collective-permute-start | bytes 589832 | tf_op jit(solution)/shard_map/ppermute | solution.py:67
  215.7 2.7 copy-start.16
  215.7 6.3 %collective-permute-start.4 = (bf16[64,1536]{1,0:T(8,128)(2,1)S(1)}, bf16[64,1536]{1,0:T(8,128)(2,1)}, u32[]{:S(2)}, u32[]{:S(2)}) collective-permute-start(bf16[64,1536]{1,0:T(8,128)(2,1)S(1)} %collective-permute-done.3), channel_id=1, source_target_pairs={{0,1},{1,2},{2,3},{3,4},{4,5},{5,6},{6,7},{7,0},{8,9},{9,10},{10,1... | collective-permute-start | bytes 589832 | tf_op jit(solution)/shard_map/ppermute | solution.py:67
  215.7 7.5 %collective-permute-start.7 = (bf16[64,1536]{1,0:T(8,128)(2,1)}, bf16[64,1536]{1,0:T(8,128)(2,1)}, u32[]{:S(2)}, u32[]{:S(2)}) collective-permute-start(bf16[64,1536]{1,0:T(8,128)(2,1)} %collective-permute-done.6), channel_id=1, source_target_pairs={{0,7},{1,0},{2,1},{3,2},{4,3},{5,4},{6,5},{7,6},{8,15},{9,8},{10,9... | collective-permute-start | bytes 589832 | tf_op jit(solution)/shard_map/ppermute | solution.py:67
  222.0 5.9 %collective-permute-start.5 = (bf16[64,1536]{1,0:T(8,128)(2,1)}, bf16[64,1536]{1,0:T(8,128)(2,1)S(1)}, u32[]{:S(2)}, u32[]{:S(2)}) collective-permute-start(bf16[64,1536]{1,0:T(8,128)(2,1)} %collective-permute-done.4), channel_id=1, source_target_pairs={{0,1},{1,2},{2,3},{3,4},{4,5},{5,6},{6,7},{7,0},{8,9},{9,10},{10,1... | collective-permute-start | bytes 589832 | tf_op jit(solution)/shard_map/ppermute | solution.py:67
  222.0 7.0 %copy-start.17 = (bf16[64,1536]{1,0:T(8,128)(2,1)S(1)}, bf16[64,1536]{1,0:T(8,128)(2,1)}, u32[]{:S(2)}) copy-start(bf16[64,1536]{1,0:T(8,128)(2,1)} %copy-done.16) | copy-start | bytes 589828
  223.1 10.9 %collective-permute-start.11 = (bf16[768,256]{1,0:T(8,128)(2,1)S(1)}, bf16[768,256]{1,0:T(8,128)(2,1)S(1)}, u32[]{:S(2)}, u32[]{:S(2)}) collective-permute-start(bf16[768,256]{1,0:T(8,128)(2,1)S(1)} %constant_dynamic-slice_fusion), channel_id=1, source_target_pairs={{0,16},{1,17},{2,18},{3,19},{4,20},{5,21},{6,22},{7,23},{8,24},{9,... | collective-permute-start | bytes 1179656 | tf_op jit(solution)/shard_map/ppermute | solution.py:67
  223.2 5.9 %collective-permute-start.8 = (bf16[64,1536]{1,0:T(8,128)(2,1)}, bf16[64,1536]{1,0:T(8,128)(2,1)S(1)}, u32[]{:S(2)}, u32[]{:S(2)}) collective-permute-start(bf16[64,1536]{1,0:T(8,128)(2,1)} %collective-permute-done.7), channel_id=1, source_target_pairs={{0,7},{1,0},{2,1},{3,2},{4,3},{5,4},{6,5},{7,6},{8,15},{9,8},{10,9... | collective-permute-start | bytes 589832 | tf_op jit(solution)/shard_map/ppermute | solution.py:67
  228.0 6.0 %copy-start.12 = (bf16[768,256]{1,0:T(8,128)(2,1)S(1)}, bf16[768,256]{1,0:T(8,128)(2,1)}, u32[]{:S(2)}) copy-start(bf16[768,256]{1,0:T(8,128)(2,1)} %copy-done.11) | copy-start | bytes 1179652
  228.0 5.9 %collective-permute-start.9 = (bf16[32,1536]{1,0:T(8,128)(2,1)S(1)}, bf16[32,1536]{1,0:T(8,128)(2,1)S(1)}, u32[]{:S(2)}, u32[]{:S(2)}) collective-permute-start(bf16[32,1536]{1,0:T(8,128)(2,1)S(1)} %slice.113), channel_id=1, source_target_pairs={{0,1},{1,2},{2,3},{3,4},{4,5},{5,6},{6,7},{7,0},{8,9},{9,10},{10,1... | collective-permute-start | bytes 294920 | tf_op jit(solution)/shard_map/ppermute | solution.py:67
  229.2 4.8 %collective-permute-start.10 = (bf16[32,1536]{1,0:T(8,128)(2,1)S(1)}, bf16[32,1536]{1,0:T(8,128)(2,1)S(1)}, u32[]{:S(2)}, u32[]{:S(2)}) collective-permute-start(bf16[32,1536]{1,0:T(8,128)(2,1)S(1)} %slice.114), channel_id=1, source_target_pairs={{0,7},{1,0},{2,1},{3,2},{4,3},{5,4},{6,5},{7,6},{8,15},{9,8},{10,9... | collective-permute-start | bytes 294920 | tf_op jit(solution)/shard_map/ppermute | solution.py:67
  234.0 1.2 copy-start.1
  236.0 10.2 %collective-permute-start.12 = (bf16[256,512]{1,0:T(8,128)(2,1)}, bf16[256,512]{1,0:T(8,128)(2,1)S(1)}, u32[]{:S(2)}, u32[]{:S(2)}) collective-permute-start(bf16[256,512]{1,0:T(8,128)(2,1)} %get-tuple-element.44), channel_id=1, source_target_pairs={{0,8},{1,9},{2,10},{3,11},{4,12},{5,13},{6,14},{7,15},{8,16},{9,17... | collective-permute-start | bytes 786440 | tf_op jit(solution)/shard_map/ppermute | solution.py:67
  237.7 1.4 copy-start.2
  239.1 2.3 copy-start.15
  239.1 5.0 %copy-start.3 = (bf16[512,1536]{1,0:T(8,128)(2,1)S(1)}, bf16[512,1536]{1,0:T(8,128)(2,1)}, u32[]{:S(2)}) copy-start(bf16[512,1536]{1,0:T(8,128)(2,1)} %copy-done.1) | copy-start | bytes 4718596
  241.4 6.0 %collective-permute-start.14 = (bf16[256,512]{1,0:T(8,128)(2,1)S(1)}, bf16[256,512]{1,0:T(8,128)(2,1)S(1)}, u32[]{:S(2)}, u32[]{:S(2)}) collective-permute-start(bf16[256,512]{1,0:T(8,128)(2,1)S(1)} %copy-done.15), channel_id=1, source_target_pairs={{0,24},{1,25},{2,26},{3,27},{4,28},{5,29},{6,30},{7,31},{8,0},{9,1... | collective-permute-start | bytes 786440 | tf_op jit(solution)/shard_map/ppermute | solution.py:67
  247.1 11.1 %collective-permute-start.13 = (bf16[512,512]{1,0:T(8,128)(2,1)}, bf16[512,512]{1,0:T(8,128)(2,1)}, u32[]{:S(2)}, u32[]{:S(2)}) collective-permute-start(bf16[512,512]{1,0:T(8,128)(2,1)} %pad_maximum_fusion.1), channel_id=1, source_target_pairs={{0,8},{1,9},{2,10},{3,11},{4,12},{5,13},{6,14},{7,15},{8,16},{9,17... | collective-permute-start | bytes 1572872 | tf_op jit(solution)/shard_map/ppermute | solution.py:67
  248.3 9.9 %collective-permute-start.15 = (bf16[512,512]{1,0:T(8,128)(2,1)}, bf16[512,512]{1,0:T(8,128)(2,1)}, u32[]{:S(2)}, u32[]{:S(2)}) collective-permute-start(bf16[512,512]{1,0:T(8,128)(2,1)} %pad_maximum_fusion.2), channel_id=1, source_target_pairs={{0,24},{1,25},{2,26},{3,27},{4,28},{5,29},{6,30},{7,31},{8,0},{9,1... | collective-permute-start | bytes 1572872 | tf_op jit(solution)/shard_map/ppermute | solution.py:67
  251.4 1.4 copy-start.4
  252.8 1.1 copy-start.7
  259.8 14.6 %copy-start.6 = (bf16[4,256,1536]{2,1,0:T(8,128)(2,1)S(1)}, bf16[4,256,1536]{2,1,0:T(8,128)(2,1)}, u32[]{:S(2)}) copy-start(bf16[4,256,1536]{2,1,0:T(8,128)(2,1)} %copy-done.5) | copy-start | bytes 9437188
  276.9 5.0 %collective-permute-start.16 = (bf16[32,1536]{1,0:T(8,128)(2,1)S(1)}, bf16[32,1536]{1,0:T(8,128)(2,1)S(1)}, u32[]{:S(2)}, u32[]{:S(2)}) collective-permute-start(bf16[32,1536]{1,0:T(8,128)(2,1)S(1)} %get-tuple-element.40), channel_id=1, source_target_pairs={{0,1},{1,2},{2,3},{3,4},{4,5},{5,6},{6,7},{7,0},{8,9},{9,10},{10,1... | collective-permute-start | bytes 294920 | tf_op jit(solution)/shard_map/ppermute | solution.py:67
  277.2 4.7 %collective-permute-start.20 = (bf16[32,1536]{1,0:T(8,128)(2,1)S(1)}, bf16[32,1536]{1,0:T(8,128)(2,1)S(1)}, u32[]{:S(2)}, u32[]{:S(2)}) collective-permute-start(bf16[32,1536]{1,0:T(8,128)(2,1)S(1)} %get-tuple-element.41), channel_id=1, source_target_pairs={{0,7},{1,0},{2,1},{3,2},{4,3},{5,4},{6,5},{7,6},{8,15},{9,8},{10,9... | collective-permute-start | bytes 294920 | tf_op jit(solution)/shard_map/ppermute | solution.py:67
  281.9 5.8 %collective-permute-start.17 = (bf16[64,1536]{1,0:T(8,128)(2,1)S(1)}, bf16[64,1536]{1,0:T(8,128)(2,1)S(1)}, u32[]{:S(2)}, u32[]{:S(2)}) collective-permute-start(bf16[64,1536]{1,0:T(8,128)(2,1)S(1)} %pad_maximum_fusion.3), channel_id=1, source_target_pairs={{0,1},{1,2},{2,3},{3,4},{4,5},{5,6},{6,7},{7,0},{8,9},{9,10},{10,1... | collective-permute-start | bytes 589832 | tf_op jit(solution)/shard_map/ppermute | solution.py:67
  282.8 5.3 %collective-permute-start.21 = (bf16[64,1536]{1,0:T(8,128)(2,1)S(1)}, bf16[64,1536]{1,0:T(8,128)(2,1)S(1)}, u32[]{:S(2)}, u32[]{:S(2)}) collective-permute-start(bf16[64,1536]{1,0:T(8,128)(2,1)S(1)} %pad_maximum_fusion.4), channel_id=1, source_target_pairs={{0,7},{1,0},{2,1},{3,2},{4,3},{5,4},{6,5},{7,6},{8,15},{9,8},{10,9... | collective-permute-start | bytes 589832 | tf_op jit(solution)/shard_map/ppermute | solution.py:67
  287.8 5.8 %collective-permute-start.18 = (bf16[64,1536]{1,0:T(8,128)(2,1)S(1)}, bf16[64,1536]{1,0:T(8,128)(2,1)S(1)}, u32[]{:S(2)}, u32[]{:S(2)}) collective-permute-start(bf16[64,1536]{1,0:T(8,128)(2,1)S(1)} %add_convert_fusion.6), channel_id=1, source_target_pairs={{0,1},{1,2},{2,3},{3,4},{4,5},{5,6},{6,7},{7,0},{8,9},{9,10},{10,1... | collective-permute-start | bytes 589832 | tf_op jit(solution)/shard_map/ppermute | solution.py:67
  293.7 34.6 %copy-start.10 = (bf16[4,6144]{1,0:T(4,128)(2,1)S(1)}, bf16[4,6144]{1,0:T(4,128)(2,1)}, u32[]{:S(2)}) copy-start(bf16[4,6144]{1,0:T(4,128)(2,1)} %param.7) | copy-start | bytes 147460
  293.7 34.6 %copy-start.14 = (f32[4,6144]{1,0:T(4,128)S(1)}, f32[4,6144]{1,0:T(4,128)}, u32[]{:S(2)}) copy-start(f32[4,6144]{1,0:T(4,128)} %copy-done.13) | copy-start | bytes 294916
  293.7 5.5 %collective-permute-start.22 = (bf16[64,1536]{1,0:T(8,128)(2,1)S(1)}, bf16[64,1536]{1,0:T(8,128)(2,1)S(1)}, u32[]{:S(2)}, u32[]{:S(2)}) collective-permute-start(bf16[64,1536]{1,0:T(8,128)(2,1)S(1)} %get-tuple-element.37), channel_id=1, source_target_pairs={{0,7},{1,0},{2,1},{3,2},{4,3},{5,4},{6,5},{7,6},{8,15},{9,8},{10,9... | collective-permute-start | bytes 589832 | tf_op jit(solution)/shard_map/ppermute | solution.py:67
  294.1 8.1 %collective-permute-start.19 = (bf16[64,1536]{1,0:T(8,128)(2,1)S(1)}, bf16[64,1536]{1,0:T(8,128)(2,1)S(1)}, u32[]{:S(2)}, u32[]{:S(2)}) collective-permute-start(bf16[64,1536]{1,0:T(8,128)(2,1)S(1)} %get-tuple-element.36), channel_id=1, source_target_pairs={{0,1},{1,2},{2,3},{3,4},{4,5},{5,6},{6,7},{7,0},{8,9},{9,10},{10,1... | collective-permute-start | bytes 589832 | tf_op jit(solution)/shard_map/ppermute | solution.py:67
  299.3 5.5 %collective-permute-start.23 = (bf16[64,1536]{1,0:T(8,128)(2,1)S(1)}, bf16[64,1536]{1,0:T(8,128)(2,1)S(1)}, u32[]{:S(2)}, u32[]{:S(2)}) collective-permute-start(bf16[64,1536]{1,0:T(8,128)(2,1)S(1)} %add_convert_fusion.3), channel_id=1, source_target_pairs={{0,7},{1,0},{2,1},{3,2},{4,3},{5,4},{6,5},{7,6},{8,15},{9,8},{10,9... | collective-permute-start | bytes 589832 | tf_op jit(solution)/shard_map/ppermute | solution.py:67
Sparse Core Ops, SparseCore 0:
  34.6 74.2 all-gather.1
  136.8 34.4 reduce-scatter.1

commit v3 on v2

--- a/solution.py
+++ b/solution.py
@@ -229,30 +229,35 @@
     )(place, rows, gate, up_parts)
 
 
-def down_product(gathered, down_parts):
-    ring, count, units = gathered.shape
-    part = down_parts.shape[2]
+def down_product(gathered, down_parts, place, far):
+    count, units = gathered[0].shape
+    ring, _, part = down_parts.shape
     columns = part // 3
 
-    def kernel(rows_ref, down_ref, out_ref):
-        total = jnp.dot(rows_ref[0], down_ref[0], preferred_element_type=F32)
-        for y in range(1, ring):
-            total = total + jnp.dot(rows_ref[y], down_ref[y], preferred_element_type=F32)
+    def kernel(place_ref, *refs):
+        rows, down_ref, out_ref = refs[:ring], refs[ring], refs[ring + 1]
+        total = None
+        for step in range(ring):
+            source = lax.rem(place_ref[0] - step + ring, ring)
+            product = jnp.dot(rows[step][...], down_ref[source], preferred_element_type=F32)
+            total = product if total is None else total + product
         out_ref[...] = total.astype(BF16)
 
     return pl.pallas_call(
         kernel,
         grid=(part // columns,),
-        in_specs=[whole_block(), pl.BlockSpec((ring, units, columns), lambda n: (0, 0, n))],
+        in_specs=[pl.BlockSpec(memory_space=pltpu.SMEM)]
+        + [whole_block()] * ring
+        + [pl.BlockSpec((ring, units, columns), lambda n: (0, 0, n))],
         out_specs=pl.BlockSpec((count, columns), lambda n: (0, n)),
-        out_shape=jax.ShapeDtypeStruct((count, part), BF16),
+        out_shape=(pltpu.HBM if far else jax.ShapeDtypeStruct)((count, part), BF16),
         compiler_params=params(16),
         cost_estimate=pl.CostEstimate(
             flops=2 * count * part * units * ring,
             bytes_accessed=2 * (ring * count * units + ring * units * part + count * part),
             transcendentals=0,
         ),
-    )(gathered, down_parts)
+    )(place, *gathered, down_parts)
 
 
 def on_device(tokens, norm_gain, gate_weight, up_weight, down_weight, expert_ids, route_weight):
@@ -278,8 +283,9 @@
         normed = rms_norm(state, norm_gain)
         return jnp.einsum("ts,td->sd", send, normed, preferred_element_type=F32).astype(BF16)
 
-    def finish(units_of, down_parts):
-        return down_product(spread(units_of, RING, "hidden", across), down_parts)
+    def finish(units_of, down_parts, far):
+        gathered = [units_of] + [shift(units_of, hidden, k, "across") for k in (1, 2, 3)]
+        return down_product(gathered, down_parts, (position // depth).reshape(1), far)
 
     def settle(summed, state):
         returned = exchange(summed.astype(BF16).reshape(experts * RING, capacity, part), both, homes)
@@ -304,7 +310,7 @@
     gathered = lax.all_gather(rows, "hidden", axis=0, tiled=True, axis_index_groups=along)
     down_parts = exchange(feature_blocks(down), "hidden", across)
     gathered, near, down_parts = lax.optimization_barrier((gathered, near, down_parts))
-    partial = finish(whole_gate_up(gathered, gate, up), down_parts)
+    partial = finish(whole_gate_up(gathered, gate, up), down_parts, True)
     partial, up_in = lax.optimization_barrier((partial, up))
     up_parts = [feature_part(up_in, position, hidden, step) for step in range(RING)]
     summed = lax.psum_scatter(
@@ -334,7 +340,7 @@
         for step in (2, 1, -1, 0)
     }
     values = ring_sum(values, 2, hidden, "across")
-    partial = finish(silu_product(values[:, :units], values[:, units:]), down_parts)
+    partial = finish(silu_product(values[:, :units], values[:, units:]), down_parts, False)
     blocks = {
         step: partial[place * block : (place + 1) * block] for place, step in enumerate(offsets)
     }

time: 337 us -> 335 us (level)
  blocking collectives: 129 us -> 103 us
  waiting for transfers between devices: 96.5 us -> 113 us
  starting transfers between devices: 45.2 us -> 53.9 us
    all_to_all x6 -> x4, blocking collectives: 129 us -> 103 us  [exchange(): lax.all_to_all(values, axis, 0, 0, tiled=True, axis_index_groups=groups)]
    ppermute x24 -> x30, waiting for transfers between devices: 84 us -> 100 us  [shift(): return lax.ppermute(values, 'hidden', shifts(hidden, step, ring))]
    ppermute x24 -> x30, starting transfers between devices: 33.6 us -> 43.1 us  [shift(): return lax.ppermute(values, 'hidden', shifts(hidden, step, ring))]
    unnamed x45 -> x43, local copies, waits for them, and re-layouts: 10.3 us -> 9.15 us
  transfers between devices with their start and end apart: 28 -> 34, of which waited for: 13 -> 17; matrix products, arithmetic and copies ran while one was open for 3% -> 3% of each run, Pallas kernels for 3% -> 3%
where the time goes in v3:
time: 335 us; the launch traced here: 334 us
  waiting for transfers between devices  113 us (34%)
  blocking collectives  103 us (31%)
  starting transfers between devices  53.9 us (16%)
  Pallas kernels  21.6 us (6%)
  local copies, waits for them, and re-layouts  20.5 us (6%)
  between operations  14 us (4%)
  other arithmetic  5.05 us (2%)
  matrix products  3.47 us (1%)
    all_to_all x4, blocking collectives, exchange(): lax.all_to_all(values, axis, 0, 0, tiled=True, axis_index_groups=groups)  103 us
    ppermute x30, waiting for transfers between devices, shift(): return lax.ppermute(values, 'hidden', shifts(hidden, step, ring))  100 us
    ppermute x30, starting transfers between devices, shift(): return lax.ppermute(values, 'hidden', shifts(hidden, step, ring))  43.1 us
    all_to_all x2, starting transfers between devices, exchange(): lax.all_to_all(values, axis, 0, 0, tiled=True, axis_index_groups=groups)  10.8 us
    unnamed x43, local copies, waits for them, and re-layouts  9.15 us
    all_to_all x2, waiting for transfers between devices, exchange(): lax.all_to_all(values, axis, 0, 0, tiled=True, axis_index_groups=groups)  8.01 us
  transfers between devices with their start and end apart: 34, of which 17 were waited for; matrix products, arithmetic and copies ran while one was open for 3% of the time, Pallas kernels for 3%

profile of v3, /device:TPU:1, one launch (start us, length us, event | category | flops | bytes accessed | tf_op | source)
XLA Modules:
  0.0 333.9 jit_solution(11089040778460965049)
XLA Ops:
  11.3 21.9 %all_to_all.30 = bf16[32,2,6144]{2,1,0:T(2,128)(2,1)S(1)} all-to-all(bf16[32,2,6144]{2,1,0:T(2,128)(2,1)S(1)} %bitcast.62), channel_id=1, replica_groups={{0,8,16,24,32,40,48,56,64,72,80,88,96,104,112,120,128,136,144,152,160,1..., dimensions={0} | all-to-all | bytes 1572864 | tf_op jit(solution)/shard_map/all_to_all | solution.py:52
  34.5 3.6 %shard_map.73 = bf16[4,256,1536]{2,1,0:T(8,128)(2,1)} custom-call(bf16[256,6144]{1,0:T(8,128)(2,1)} %bitcast.61), custom_call_target="tpu_custom_call" | custom-call | bytes 6291456 | tf_op jit(solution)/shard_map/pallas_call | solution.py:195
  38.1 3.7 %all-to-all-start.1 = ((bf16[4,256,1536]{2,1,0:T(8,128)(2,1)}), bf16[4,256,1536]{2,1,0:T(8,128)(2,1)S(1)}, u32[]{:S(2)}, u32[]{:S(2)}) async-start(bf16[4,256,1536]{2,1,0:T(8,128)(2,1)} %shard_map.73), calls=%async_computation.1 | async-start | bytes 6291456 | tf_op jit(solution)/shard_map/all_to_all | solution.py:52
  41.9 3.1 dynamic-slice_bitcast_fusion
  45.0 1.3 collective-permute-start
  46.3 1.4 collective-permute-start.1
  48.7 1.7 collective-permute-start.2
  50.4 53.2 %collective-permute-done.2 = bf16[768,256]{1,0:T(8,128)(2,1)S(1)} collective-permute-done((bf16[768,256]{1,0:T(8,128)(2,1)S(1)}, bf16[768,256]{1,0:T(8,128)(2,1)S(1)}, u32[]{:S(2)}, u32[]{:S(2)}) %collective-permute-start.2) | collective-permute-done | bytes 393248 | tf_op jit(solution)/shard_map/ppermute | solution.py:67
  104.4 4.6 %all-gather.2.cloned.1.call-done.rows_hbm = bf16[512,6144]{1,0:T(8,128)(2,1)} async-done(((bf16[64,6144]{1,0:T(8,128)(2,1)}), bf16[512,6144]{1,0:T(8,128)(2,1)}) %all-gather.2.cloned.1.call-update) | async-done | bytes 6291472 | tf_op jit(solution)/shard_map/all_gather | solution.py:310
  108.9 6.0 %shard_map.74.refs_0_ = bf16[512,256]{1,0:T(8,128)(2,1)S(1)} custom-call(bf16[512,6144]{1,0:T(8,128)(2,1)} %all-gather.2.cloned.1.call-done.rows_hbm, bf16[6144,256]{1,0:T(8,128)(2,1)} %bitcast.59, bf16[6144,256]{1,0:T(8,128)(2,1)} %bitcast.57), custom_call_target="tpu_custom_call" | custom-call | flops 3221225472 | bytes 12582912 | tf_op jit(solution)/shard_map/pallas_call | solution.py:159
  116.2 2.4 collective-permute-start.4
  119.8 3.6 %collective-permute-done.3.refs_1_ = bf16[512,256]{1,0:T(8,128)(2,1)S(1)} collective-permute-done((bf16[512,256]{1,0:T(8,128)(2,1)S(1)}, bf16[512,256]{1,0:T(8,128)(2,1)S(1)}, u32[]{:S(2)}, u32[]{:S(2)}) %collective-permute-start.3) | collective-permute-done | bytes 262176 | tf_op jit(solution)/shard_map/ppermute | solution.py:67
  123.4 6.6 %collective-permute-done.4.refs_2_ = bf16[512,256]{1,0:T(8,128)(2,1)S(1)} collective-permute-done((bf16[512,256]{1,0:T(8,128)(2,1)S(1)}, bf16[512,256]{1,0:T(8,128)(2,1)S(1)}, u32[]{:S(2)}, u32[]{:S(2)}) %collective-permute-start.4) | collective-permute-done | bytes 262176 | tf_op jit(solution)/shard_map/ppermute | solution.py:67
  130.0 3.3 shard_map.75
  133.3 40.9 %all_to_all.31.up_ref = bf16[4,1536,256]{2,1,0:T(8,128)(2,1)S(1)} all-to-all(bf16[4,1536,256]{2,1,0:T(8,128)(2,1)} %bitcast.58), channel_id=1, replica_groups={{0,8,16,24},{1,9,17,25},{2,10,18,26},{3,11,19,27},{4,12,20,28},{5,13,21..., dimensions={0} | all-to-all | bytes 6291456 | tf_op jit(solution)/shard_map/all_to_all | solution.py:52
  174.2 1.7 reshape.92
  175.9 7.1 %all-to-all-start.3 = ((bf16[32,2,1536]{2,1,0:T(2,128)(2,1)}), bf16[32,2,1536]{2,1,0:T(2,128)(2,1)S(1)}, u32[]{:S(2)}, u32[]{:S(2)}) async-start(bf16[32,2,1536]{2,1,0:T(2,128)(2,1)} %reshape.92), calls=%async_computation.4 | async-start | bytes 393216 | tf_op jit(solution)/shard_map/all_to_all | solution.py:52
  183.2 8.0 %all-to-all-done.3 = bf16[32,2,1536]{2,1,0:T(2,128)(2,1)S(1)} async-done(((bf16[32,2,1536]{2,1,0:T(2,128)(2,1)}), bf16[32,2,1536]{2,1,0:T(2,128)(2,1)S(1)}, u32[]{:S(2)}, u32[]{:S(2)}) %all-to-all-start.3) | async-done | bytes 196640 | tf_op jit(solution)/shard_map/all_to_all | solution.py:52
  193.7 12.1 %all_to_all.32 = bf16[32,2,1536]{2,1,0:T(2,128)(2,1)S(1)} all-to-all(bf16[32,2,1536]{2,1,0:T(2,128)(2,1)S(1)} %bitcast.66), channel_id=1, replica_groups={{0,8,16,24,32,40,48,56,64,72,80,88,96,104,112,120,128,136,144,152,160,1..., dimensions={0} | all-to-all | bytes 393216 | tf_op jit(solution)/shard_map/all_to_all | solution.py:52
  206.1 2.7 collective-permute-start.9
  208.8 4.5 %collective-permute-done.6 = bf16[64,1536]{1,0:T(8,128)(2,1)S(1)} collective-permute-done((bf16[64,1536]{1,0:T(8,128)(2,1)S(1)}, bf16[64,1536]{1,0:T(8,128)(2,1)S(1)}, u32[]{:S(2)}, u32[]{:S(2)}) %collective-permute-start.6) | collective-permute-done | bytes 196640 | tf_op jit(solution)/shard_map/ppermute | solution.py:67
  213.2 2.7 collective-permute-start.10
  215.9 3.6 %collective-permute-done.7 = bf16[64,1536]{1,0:T(8,128)(2,1)} collective-permute-done((bf16[64,1536]{1,0:T(8,128)(2,1)S(1)}, bf16[64,1536]{1,0:T(8,128)(2,1)}, u32[]{:S(2)}, u32[]{:S(2)}) %collective-permute-start.7) | collective-permute-done | bytes 196640 | tf_op jit(solution)/shard_map/ppermute | solution.py:67
  220.7 2.7 collective-permute-start.11
  223.5 2.0 collective-permute-done.8
  226.7 2.9 collective-permute-start.13
  233.5 1.7 collective-permute-start.15
  235.2 1.4 copy-done.2
  236.6 2.2 shard_map.77
  238.9 2.7 collective-permute-start.17
  241.6 2.1 shard_map.79
  245.8 3.1 collective-permute-start.18
  248.9 1.4 copy-done.4
  252.4 3.3 collective-permute-done.16
  255.7 1.4 convert_add_fusion
  258.3 3.7 %collective-permute-start.20 = (bf16[512,256]{1,0:T(8,128)(2,1)S(1)}, bf16[512,256]{1,0:T(8,128)(2,1)S(1)}, u32[]{:S(2)}, u32[]{:S(2)}) collective-permute-start(bf16[512,256]{1,0:T(8,128)(2,1)S(1)} %fusion.9.refs_0_), channel_id=1, source_target_pairs={{0,16},{1,17},{2,18},{3,19},{4,20},{5,21},{6,22},{7,23},{8,24},{9,... | collective-permute-start | bytes 786440 | tf_op jit(solution)/shard_map/ppermute | solution.py:67
  262.2 2.4 collective-permute-done.19.refs_1_
  264.6 4.1 %collective-permute-done.20.refs_2_ = bf16[512,256]{1,0:T(8,128)(2,1)S(1)} collective-permute-done((bf16[512,256]{1,0:T(8,128)(2,1)S(1)}, bf16[512,256]{1,0:T(8,128)(2,1)S(1)}, u32[]{:S(2)}, u32[]{:S(2)}) %collective-permute-start.20) | collective-permute-done | bytes 262176 | tf_op jit(solution)/shard_map/ppermute | solution.py:67
  268.7 2.5 shard_map.80
  271.3 2.7 collective-permute-start.26
  273.9 2.0 collective-permute-done.22
  276.3 2.5 collective-permute-start.27
  278.9 2.9 collective-permute-done.23
  282.0 5.7 %collective-permute-done.24 = bf16[64,1536]{1,0:T(8,128)(2,1)S(1)} collective-permute-done((bf16[64,1536]{1,0:T(8,128)(2,1)S(1)}, bf16[64,1536]{1,0:T(8,128)(2,1)S(1)}, u32[]{:S(2)}, u32[]{:S(2)}) %collective-permute-start.24) | collective-permute-done | bytes 196640 | tf_op jit(solution)/shard_map/ppermute | solution.py:67
  289.3 3.2 collective-permute-done.28
  292.6 2.8 collective-permute-start.29
  295.4 2.6 collective-permute-done.29
  298.2 27.9 %all_to_all.33 = bf16[32,2,1536]{2,1,0:T(2,128)(2,1)S(1)} all-to-all(bf16[32,2,1536]{2,1,0:T(2,128)(2,1)S(1)} %reshape.101), channel_id=1, replica_groups={{0,8,16,24,32,40,48,56,64,72,80,88,96,104,112,120,128,136,144,152,160,1..., dimensions={0} | all-to-all | bytes 393216 | tf_op jit(solution)/shard_map/all_to_all | solution.py:52
  (128 shorter events, 28.5 us)
Async XLA Ops:
  6.5 102.4 %all-gather.2.cloned.1.call-start = ((), (), s32[]{:S(2)}) async-start(), calls=%async_computation.7 | async-start | bytes 7077888 | tf_op jit(solution)/shard_map/all_gather | solution.py:310
  38.1 66.3 %all-to-all-start.1 = ((bf16[4,256,1536]{2,1,0:T(8,128)(2,1)}), bf16[4,256,1536]{2,1,0:T(8,128)(2,1)S(1)}, u32[]{:S(2)}, u32[]{:S(2)}) async-start(bf16[4,256,1536]{2,1,0:T(8,128)(2,1)} %shard_map.73), calls=%async_computation.1 | async-start | bytes 6291456 | tf_op jit(solution)/shard_map/all_to_all | solution.py:52
  41.8 132.4 %reduce-scatter.2.cloned.1.call-start = ((), (), s32[]{:S(2)}) async-start(), calls=%async_computation.8 | async-start | bytes 1769472 | tf_op jit(solution)/shard_map/reduce_scatter | solution.py:316
  45.0 58.6 %collective-permute-start = (bf16[1536,256]{1,0:T(8,128)(2,1)}, bf16[1536,256]{1,0:T(8,128)(2,1)}, u32[]{:S(2)}, u32[]{:S(2)}) collective-permute-start(bf16[1536,256]{1,0:T(8,128)(2,1)} %get-tuple-element.35), channel_id=1, source_target_pairs={{0,8},{1,9},{2,10},{3,11},{4,12},{5,13},{6,14},{7,15},{8,16},{9,17... | collective-permute-start | bytes 2359304 | tf_op jit(solution)/shard_map/ppermute | solution.py:67
  46.3 58.1 %collective-permute-start.1 = (bf16[1536,256]{1,0:T(8,128)(2,1)}, bf16[1536,256]{1,0:T(8,128)(2,1)}, u32[]{:S(2)}, u32[]{:S(2)}) collective-permute-start(bf16[1536,256]{1,0:T(8,128)(2,1)} %get-tuple-element.34), channel_id=1, source_target_pairs={{0,24},{1,25},{2,26},{3,27},{4,28},{5,29},{6,30},{7,31},{8,0},{9,1... | collective-permute-start | bytes 2359304 | tf_op jit(solution)/shard_map/ppermute | solution.py:67
  48.7 54.9 %collective-permute-start.2 = (bf16[768,256]{1,0:T(8,128)(2,1)S(1)}, bf16[768,256]{1,0:T(8,128)(2,1)S(1)}, u32[]{:S(2)}, u32[]{:S(2)}) collective-permute-start(bf16[768,256]{1,0:T(8,128)(2,1)S(1)} %dynamic-slice_bitcast_fusion.3), channel_id=1, source_target_pairs={{0,16},{1,17},{2,18},{3,19},{4,20},{5,21},{6,22},{7,23},{8,24},{9,... | collective-permute-start | bytes 1179656 | tf_op jit(solution)/shard_map/ppermute | solution.py:67
  104.4 25.6 %copy-start.5 = (bf16[4,256,1536]{2,1,0:T(8,128)(2,1)}, bf16[4,256,1536]{2,1,0:T(8,128)(2,1)S(1)}, u32[]{:S(2)}) copy-start(bf16[4,256,1536]{2,1,0:T(8,128)(2,1)S(1)} %all-to-all-done.1.refs_4_) | copy-start | bytes 9437188
  114.9 8.5 %collective-permute-start.3 = (bf16[512,256]{1,0:T(8,128)(2,1)S(1)}, bf16[512,256]{1,0:T(8,128)(2,1)S(1)}, u32[]{:S(2)}, u32[]{:S(2)}) collective-permute-start(bf16[512,256]{1,0:T(8,128)(2,1)S(1)} %shard_map.74.refs_0_), channel_id=1, source_target_pairs={{0,8},{1,9},{2,10},{3,11},{4,12},{5,13},{6,14},{7,15},{8,16},{9,17... | collective-permute-start | bytes 786440 | tf_op jit(solution)/shard_map/ppermute | solution.py:67
  116.2 13.8 %collective-permute-start.4 = (bf16[512,256]{1,0:T(8,128)(2,1)S(1)}, bf16[512,256]{1,0:T(8,128)(2,1)S(1)}, u32[]{:S(2)}, u32[]{:S(2)}) collective-permute-start(bf16[512,256]{1,0:T(8,128)(2,1)S(1)} %shard_map.74.refs_0_), channel_id=1, source_target_pairs={{0,16},{1,17},{2,18},{3,19},{4,20},{5,21},{6,22},{7,23},{8,24},{9,... | collective-permute-start | bytes 786440 | tf_op jit(solution)/shard_map/ppermute | solution.py:67
  118.7 11.3 %collective-permute-start.5 = (bf16[512,256]{1,0:T(8,128)(2,1)S(1)}, bf16[512,256]{1,0:T(8,128)(2,1)S(1)}, u32[]{:S(2)}, u32[]{:S(2)}) collective-permute-start(bf16[512,256]{1,0:T(8,128)(2,1)S(1)} %shard_map.74.refs_0_), channel_id=1, source_target_pairs={{0,24},{1,25},{2,26},{3,27},{4,28},{5,29},{6,30},{7,31},{8,0},{9,1... | collective-permute-start | bytes 786440 | tf_op jit(solution)/shard_map/ppermute | solution.py:67
  133.3 58.0 %copy-start.8 = (bf16[4,6144]{1,0:T(4,128)(2,1)S(1)}, bf16[4,6144]{1,0:T(4,128)(2,1)}, u32[]{:S(2)}) copy-start(bf16[4,6144]{1,0:T(4,128)(2,1)} %param.7) | copy-start | bytes 147460
  175.9 15.3 %all-to-all-start.3 = ((bf16[32,2,1536]{2,1,0:T(2,128)(2,1)}), bf16[32,2,1536]{2,1,0:T(2,128)(2,1)S(1)}, u32[]{:S(2)}, u32[]{:S(2)}) async-start(bf16[32,2,1536]{2,1,0:T(2,128)(2,1)} %reshape.92), calls=%async_computation.4 | async-start | bytes 393216 | tf_op jit(solution)/shard_map/all_to_all | solution.py:52
  205.8 7.4 %collective-permute-start.6 = (bf16[64,1536]{1,0:T(8,128)(2,1)S(1)}, bf16[64,1536]{1,0:T(8,128)(2,1)S(1)}, u32[]{:S(2)}, u32[]{:S(2)}) collective-permute-start(bf16[64,1536]{1,0:T(8,128)(2,1)S(1)} %reshape.97), channel_id=1, source_target_pairs={{0,1},{1,2},{2,3},{3,4},{4,5},{5,6},{6,7},{7,0},{8,9},{9,10},{10,1... | collective-permute-start | bytes 589832 | tf_op jit(solution)/shard_map/ppermute | solution.py:67
  206.1 7.1 %collective-permute-start.9 = (bf16[64,1536]{1,0:T(8,128)(2,1)S(1)}, bf16[64,1536]{1,0:T(8,128)(2,1)}, u32[]{:S(2)}, u32[]{:S(2)}) collective-permute-start(bf16[64,1536]{1,0:T(8,128)(2,1)S(1)} %reshape.97), channel_id=1, source_target_pairs={{0,7},{1,0},{2,1},{3,2},{4,3},{5,4},{6,5},{7,6},{8,15},{9,8},{10,9... | collective-permute-start | bytes 589832 | tf_op jit(solution)/shard_map/ppermute | solution.py:67
  213.2 2.7 copy-start.15
  213.2 6.3 %collective-permute-start.7 = (bf16[64,1536]{1,0:T(8,128)(2,1)S(1)}, bf16[64,1536]{1,0:T(8,128)(2,1)}, u32[]{:S(2)}, u32[]{:S(2)}) collective-permute-start(bf16[64,1536]{1,0:T(8,128)(2,1)S(1)} %collective-permute-done.6), channel_id=1, source_target_pairs={{0,1},{1,2},{2,3},{3,4},{4,5},{5,6},{6,7},{7,0},{8,9},{9,10},{10,1... | collective-permute-start | bytes 589832 | tf_op jit(solution)/shard_map/ppermute | solution.py:67
  213.2 7.5 %collective-permute-start.10 = (bf16[64,1536]{1,0:T(8,128)(2,1)}, bf16[64,1536]{1,0:T(8,128)(2,1)}, u32[]{:S(2)}, u32[]{:S(2)}) collective-permute-start(bf16[64,1536]{1,0:T(8,128)(2,1)} %collective-permute-done.9), channel_id=1, source_target_pairs={{0,7},{1,0},{2,1},{3,2},{4,3},{5,4},{6,5},{7,6},{8,15},{9,8},{10,9... | collective-permute-start | bytes 589832 | tf_op jit(solution)/shard_map/ppermute | solution.py:67
  219.5 5.9 %collective-permute-start.8 = (bf16[64,1536]{1,0:T(8,128)(2,1)}, bf16[64,1536]{1,0:T(8,128)(2,1)S(1)}, u32[]{:S(2)}, u32[]{:S(2)}) collective-permute-start(bf16[64,1536]{1,0:T(8,128)(2,1)} %collective-permute-done.7), channel_id=1, source_target_pairs={{0,1},{1,2},{2,3},{3,4},{4,5},{5,6},{6,7},{7,0},{8,9},{9,10},{10,1... | collective-permute-start | bytes 589832 | tf_op jit(solution)/shard_map/ppermute | solution.py:67
  219.5 7.0 %copy-start.16 = (bf16[64,1536]{1,0:T(8,128)(2,1)S(1)}, bf16[64,1536]{1,0:T(8,128)(2,1)}, u32[]{:S(2)}) copy-start(bf16[64,1536]{1,0:T(8,128)(2,1)} %copy-done.15) | copy-start | bytes 589828
  220.6 10.9 %collective-permute-start.14 = (bf16[768,256]{1,0:T(8,128)(2,1)S(1)}, bf16[768,256]{1,0:T(8,128)(2,1)S(1)}, u32[]{:S(2)}, u32[]{:S(2)}) collective-permute-start(bf16[768,256]{1,0:T(8,128)(2,1)S(1)} %constant_dynamic-slice_fusion), channel_id=1, source_target_pairs={{0,16},{1,17},{2,18},{3,19},{4,20},{5,21},{6,22},{7,23},{8,24},{9,... | collective-permute-start | bytes 1179656 | tf_op jit(solution)/shard_map/ppermute | solution.py:67
  220.7 5.9 %collective-permute-start.11 = (bf16[64,1536]{1,0:T(8,128)(2,1)}, bf16[64,1536]{1,0:T(8,128)(2,1)S(1)}, u32[]{:S(2)}, u32[]{:S(2)}) collective-permute-start(bf16[64,1536]{1,0:T(8,128)(2,1)} %collective-permute-done.10), channel_id=1, source_target_pairs={{0,7},{1,0},{2,1},{3,2},{4,3},{5,4},{6,5},{7,6},{8,15},{9,8},{10,9... | collective-permute-start | bytes 589832 | tf_op jit(solution)/shard_map/ppermute | solution.py:67
  225.5 6.0 %copy-start.11 = (bf16[768,256]{1,0:T(8,128)(2,1)S(1)}, bf16[768,256]{1,0:T(8,128)(2,1)}, u32[]{:S(2)}) copy-start(bf16[768,256]{1,0:T(8,128)(2,1)} %copy-done.10) | copy-start | bytes 1179652
  225.5 5.9 %collective-permute-start.12 = (bf16[32,1536]{1,0:T(8,128)(2,1)S(1)}, bf16[32,1536]{1,0:T(8,128)(2,1)S(1)}, u32[]{:S(2)}, u32[]{:S(2)}) collective-permute-start(bf16[32,1536]{1,0:T(8,128)(2,1)S(1)} %slice.113), channel_id=1, source_target_pairs={{0,1},{1,2},{2,3},{3,4},{4,5},{5,6},{6,7},{7,0},{8,9},{9,10},{10,1... | collective-permute-start | bytes 294920 | tf_op jit(solution)/shard_map/ppermute | solution.py:67
  226.7 4.8 %collective-permute-start.13 = (bf16[32,1536]{1,0:T(8,128)(2,1)S(1)}, bf16[32,1536]{1,0:T(8,128)(2,1)S(1)}, u32[]{:S(2)}, u32[]{:S(2)}) collective-permute-start(bf16[32,1536]{1,0:T(8,128)(2,1)S(1)} %slice.114), channel_id=1, source_target_pairs={{0,7},{1,0},{2,1},{3,2},{4,3},{5,4},{6,5},{7,6},{8,15},{9,8},{10,9... | collective-permute-start | bytes 294920 | tf_op jit(solution)/shard_map/ppermute | solution.py:67
  231.5 1.2 copy-start.1
  233.5 10.2 %collective-permute-start.15 = (bf16[256,512]{1,0:T(8,128)(2,1)}, bf16[256,512]{1,0:T(8,128)(2,1)S(1)}, u32[]{:S(2)}, u32[]{:S(2)}) collective-permute-start(bf16[256,512]{1,0:T(8,128)(2,1)} %get-tuple-element.44), channel_id=1, source_target_pairs={{0,8},{1,9},{2,10},{3,11},{4,12},{5,13},{6,14},{7,15},{8,16},{9,17... | collective-permute-start | bytes 786440 | tf_op jit(solution)/shard_map/ppermute | solution.py:67
  235.2 1.4 copy-start.2
  236.6 2.3 copy-start.14
  236.6 5.0 %copy-start.3 = (bf16[512,1536]{1,0:T(8,128)(2,1)S(1)}, bf16[512,1536]{1,0:T(8,128)(2,1)}, u32[]{:S(2)}) copy-start(bf16[512,1536]{1,0:T(8,128)(2,1)} %copy-done.1) | copy-start | bytes 4718596
  238.9 6.0 %collective-permute-start.17 = (bf16[256,512]{1,0:T(8,128)(2,1)S(1)}, bf16[256,512]{1,0:T(8,128)(2,1)S(1)}, u32[]{:S(2)}, u32[]{:S(2)}) collective-permute-start(bf16[256,512]{1,0:T(8,128)(2,1)S(1)} %copy-done.14), channel_id=1, source_target_pairs={{0,24},{1,25},{2,26},{3,27},{4,28},{5,29},{6,30},{7,31},{8,0},{9,1... | collective-permute-start | bytes 786440 | tf_op jit(solution)/shard_map/ppermute | solution.py:67
  244.6 11.1 %collective-permute-start.16 = (bf16[512,512]{1,0:T(8,128)(2,1)}, bf16[512,512]{1,0:T(8,128)(2,1)}, u32[]{:S(2)}, u32[]{:S(2)}) collective-permute-start(bf16[512,512]{1,0:T(8,128)(2,1)} %pad_maximum_fusion.1), channel_id=1, source_target_pairs={{0,8},{1,9},{2,10},{3,11},{4,12},{5,13},{6,14},{7,15},{8,16},{9,17... | collective-permute-start | bytes 1572872 | tf_op jit(solution)/shard_map/ppermute | solution.py:67
  245.8 10.0 %collective-permute-start.18 = (bf16[512,512]{1,0:T(8,128)(2,1)}, bf16[512,512]{1,0:T(8,128)(2,1)}, u32[]{:S(2)}, u32[]{:S(2)}) collective-permute-start(bf16[512,512]{1,0:T(8,128)(2,1)} %pad_maximum_fusion.2), channel_id=1, source_target_pairs={{0,24},{1,25},{2,26},{3,27},{4,28},{5,29},{6,30},{7,31},{8,0},{9,1... | collective-permute-start | bytes 1572872 | tf_op jit(solution)/shard_map/ppermute | solution.py:67
  248.9 1.4 copy-start.4
  250.3 1.1 copy-start.7
  252.4 16.3 %copy-start.6 = (bf16[4,256,1536]{2,1,0:T(8,128)(2,1)S(1)}, bf16[4,256,1536]{2,1,0:T(8,128)(2,1)}, u32[]{:S(2)}) copy-start(bf16[4,256,1536]{2,1,0:T(8,128)(2,1)} %copy-done.5) | copy-start | bytes 9437188
  257.3 7.2 %collective-permute-start.19 = (bf16[512,256]{1,0:T(8,128)(2,1)S(1)}, bf16[512,256]{1,0:T(8,128)(2,1)S(1)}, u32[]{:S(2)}, u32[]{:S(2)}) collective-permute-start(bf16[512,256]{1,0:T(8,128)(2,1)S(1)} %fusion.9.refs_0_), channel_id=1, source_target_pairs={{0,8},{1,9},{2,10},{3,11},{4,12},{5,13},{6,14},{7,15},{8,16},{9,17... | collective-permute-start | bytes 786440 | tf_op jit(solution)/shard_map/ppermute | solution.py:67
  258.3 10.3 %collective-permute-start.20 = (bf16[512,256]{1,0:T(8,128)(2,1)S(1)}, bf16[512,256]{1,0:T(8,128)(2,1)S(1)}, u32[]{:S(2)}, u32[]{:S(2)}) collective-permute-start(bf16[512,256]{1,0:T(8,128)(2,1)S(1)} %fusion.9.refs_0_), channel_id=1, source_target_pairs={{0,16},{1,17},{2,18},{3,19},{4,20},{5,21},{6,22},{7,23},{8,24},{9,... | collective-permute-start | bytes 786440 | tf_op jit(solution)/shard_map/ppermute | solution.py:67
  262.0 6.7 %collective-permute-start.21 = (bf16[512,256]{1,0:T(8,128)(2,1)S(1)}, bf16[512,256]{1,0:T(8,128)(2,1)S(1)}, u32[]{:S(2)}, u32[]{:S(2)}) collective-permute-start(bf16[512,256]{1,0:T(8,128)(2,1)S(1)} %fusion.9.refs_0_), channel_id=1, source_target_pairs={{0,24},{1,25},{2,26},{3,27},{4,28},{5,29},{6,30},{7,31},{8,0},{9,1... | collective-permute-start | bytes 786440 | tf_op jit(solution)/shard_map/ppermute | solution.py:67
  271.2 4.8 %collective-permute-start.22 = (bf16[32,1536]{1,0:T(8,128)(2,1)S(1)}, bf16[32,1536]{1,0:T(8,128)(2,1)S(1)}, u32[]{:S(2)}, u32[]{:S(2)}) collective-permute-start(bf16[32,1536]{1,0:T(8,128)(2,1)S(1)} %get-tuple-element.40), channel_id=1, source_target_pairs={{0,1},{1,2},{2,3},{3,4},{4,5},{5,6},{6,7},{7,0},{8,9},{9,10},{10,1... | collective-permute-start | bytes 294920 | tf_op jit(solution)/shard_map/ppermute | solution.py:67
  271.3 4.7 %collective-permute-start.26 = (bf16[32,1536]{1,0:T(8,128)(2,1)S(1)}, bf16[32,1536]{1,0:T(8,128)(2,1)S(1)}, u32[]{:S(2)}, u32[]{:S(2)}) collective-permute-start(bf16[32,1536]{1,0:T(8,128)(2,1)S(1)} %get-tuple-element.41), channel_id=1, source_target_pairs={{0,7},{1,0},{2,1},{3,2},{4,3},{5,4},{6,5},{7,6},{8,15},{9,8},{10,9... | collective-permute-start | bytes 294920 | tf_op jit(solution)/shard_map/ppermute | solution.py:67
  276.0 5.8 %collective-permute-start.23 = (bf16[64,1536]{1,0:T(8,128)(2,1)S(1)}, bf16[64,1536]{1,0:T(8,128)(2,1)S(1)}, u32[]{:S(2)}, u32[]{:S(2)}) collective-permute-start(bf16[64,1536]{1,0:T(8,128)(2,1)S(1)} %pad_maximum_fusion.3), channel_id=1, source_target_pairs={{0,1},{1,2},{2,3},{3,4},{4,5},{5,6},{6,7},{7,0},{8,9},{9,10},{10,1... | collective-permute-start | bytes 589832 | tf_op jit(solution)/shard_map/ppermute | solution.py:67
  276.3 5.6 %collective-permute-start.27 = (bf16[64,1536]{1,0:T(8,128)(2,1)S(1)}, bf16[64,1536]{1,0:T(8,128)(2,1)S(1)}, u32[]{:S(2)}, u32[]{:S(2)}) collective-permute-start(bf16[64,1536]{1,0:T(8,128)(2,1)S(1)} %pad_maximum_fusion.4), channel_id=1, source_target_pairs={{0,7},{1,0},{2,1},{3,2},{4,3},{5,4},{6,5},{7,6},{8,15},{9,8},{10,9... | collective-permute-start | bytes 589832 | tf_op jit(solution)/shard_map/ppermute | solution.py:67
  281.9 5.8 %collective-permute-start.24 = (bf16[64,1536]{1,0:T(8,128)(2,1)S(1)}, bf16[64,1536]{1,0:T(8,128)(2,1)S(1)}, u32[]{:S(2)}, u32[]{:S(2)}) collective-permute-start(bf16[64,1536]{1,0:T(8,128)(2,1)S(1)} %add_convert_fusion.6), channel_id=1, source_target_pairs={{0,1},{1,2},{2,3},{3,4},{4,5},{5,6},{6,7},{7,0},{8,9},{9,10},{10,1... | collective-permute-start | bytes 589832 | tf_op jit(solution)/shard_map/ppermute | solution.py:67
  287.8 38.4 %copy-start.9 = (bf16[4,6144]{1,0:T(4,128)(2,1)S(1)}, bf16[4,6144]{1,0:T(4,128)(2,1)}, u32[]{:S(2)}) copy-start(bf16[4,6144]{1,0:T(4,128)(2,1)} %param.7) | copy-start | bytes 147460
  287.8 38.4 %copy-start.13 = (f32[4,6144]{1,0:T(4,128)S(1)}, f32[4,6144]{1,0:T(4,128)}, u32[]{:S(2)}) copy-start(f32[4,6144]{1,0:T(4,128)} %copy-done.12) | copy-start | bytes 294916
  287.8 4.7 %collective-permute-start.28 = (bf16[64,1536]{1,0:T(8,128)(2,1)S(1)}, bf16[64,1536]{1,0:T(8,128)(2,1)S(1)}, u32[]{:S(2)}, u32[]{:S(2)}) collective-permute-start(bf16[64,1536]{1,0:T(8,128)(2,1)S(1)} %get-tuple-element.37), channel_id=1, source_target_pairs={{0,7},{1,0},{2,1},{3,2},{4,3},{5,4},{6,5},{7,6},{8,15},{9,8},{10,9... | collective-permute-start | bytes 589832 | tf_op jit(solution)/shard_map/ppermute | solution.py:67
  288.1 7.3 %collective-permute-start.25 = (bf16[64,1536]{1,0:T(8,128)(2,1)S(1)}, bf16[64,1536]{1,0:T(8,128)(2,1)S(1)}, u32[]{:S(2)}, u32[]{:S(2)}) collective-permute-start(bf16[64,1536]{1,0:T(8,128)(2,1)S(1)} %get-tuple-element.36), channel_id=1, source_target_pairs={{0,1},{1,2},{2,3},{3,4},{4,5},{5,6},{6,7},{7,0},{8,9},{9,10},{10,1... | collective-permute-start | bytes 589832 | tf_op jit(solution)/shard_map/ppermute | solution.py:67
  292.6 5.5 %collective-permute-start.29 = (bf16[64,1536]{1,0:T(8,128)(2,1)S(1)}, bf16[64,1536]{1,0:T(8,128)(2,1)S(1)}, u32[]{:S(2)}, u32[]{:S(2)}) collective-permute-start(bf16[64,1536]{1,0:T(8,128)(2,1)S(1)} %add_convert_fusion.3), channel_id=1, source_target_pairs={{0,7},{1,0},{2,1},{3,2},{4,3},{5,4},{6,5},{7,6},{8,15},{9,8},{10,9... | collective-permute-start | bytes 589832 | tf_op jit(solution)/shard_map/ppermute | solution.py:67
  (3 other events, 2.1 us)
Sparse Core Ops, SparseCore 0:
  34.6 74.2 all-gather.1
  133.4 35.6 reduce-scatter.1

commit v4 on v3

--- a/solution.py
+++ b/solution.py
@@ -218,8 +218,9 @@
     return pl.pallas_call(
         kernel,
         in_specs=[pl.BlockSpec(memory_space=pltpu.SMEM)] + [whole_block()] * 3,
-        out_specs=whole_block(),
-        out_shape=jax.ShapeDtypeStruct((count, 2 * units), BF16),
+        grid=(1,),
+        out_specs=pl.BlockSpec((count, 2 * units), lambda step: (0, 0)),
+        out_shape=pltpu.HBM((count, 2 * units), BF16),
         compiler_params=pltpu.CompilerParams(vmem_limit_bytes=8 * 1024 * 1024),
         cost_estimate=pl.CostEstimate(
             flops=4 * count * part * units,

time: 335 us -> 334 us (level)
  blocking collectives: 103 us -> 99.6 us
    unnamed x43 -> x49, local copies, waits for them, and re-layouts: 9.15 us -> 9.16 us
  transfers between devices with their start and end apart: 34 -> 34, of which waited for: 17 -> 16; matrix products, arithmetic and copies ran while one was open for 3% -> 3% of each run, Pallas kernels for 3% -> 3%
where the time goes in v4:
time: 334 us; the launch traced here: 333 us
  waiting for transfers between devices  112 us (34%)
  blocking collectives  99.6 us (30%)
  starting transfers between devices  52.4 us (16%)
  Pallas kernels  24.8 us (7%)
  local copies, waits for them, and re-layouts  21.7 us (6%)
  between operations  13.9 us (4%)
  other arithmetic  5.15 us (2%)
    ppermute x30, waiting for transfers between devices, shift(): return lax.ppermute(values, 'hidden', shifts(hidden, step, ring))  99.7 us
    all_to_all x4, blocking collectives, exchange(): lax.all_to_all(values, axis, 0, 0, tiled=True, axis_index_groups=groups)  99.6 us
    ppermute x30, starting transfers between devices, shift(): return lax.ppermute(values, 'hidden', shifts(hidden, step, ring))  41.5 us
    all_to_all x2, starting transfers between devices, exchange(): lax.all_to_all(values, axis, 0, 0, tiled=True, axis_index_groups=groups)  10.8 us
    pallas_call x4, Pallas kernels, part_gate_up(): pl.pallas_call(kernel, in_specs=[pl.BlockSpec(memory_space=pltpu.SMEM)] +...  9.53 us
    unnamed x49, local copies, waits for them, and re-layouts  9.16 us
    all_to_all x2, waiting for transfers between devices, exchange(): lax.all_to_all(values, axis, 0, 0, tiled=True, axis_index_groups=groups)  8.01 us
  transfers between devices with their start and end apart: 34, of which 16 were waited for; matrix products, arithmetic and copies ran while one was open for 3% of the time, Pallas kernels for 3%

profile of v4, /device:TPU:1, one launch (start us, length us, event | category | flops | bytes accessed | tf_op | source)
XLA Modules:
  0.0 332.6 jit_solution(16157533012621983452)
XLA Ops:
  11.3 21.9 %all_to_all.30 = bf16[32,2,6144]{2,1,0:T(2,128)(2,1)S(1)} all-to-all(bf16[32,2,6144]{2,1,0:T(2,128)(2,1)S(1)} %bitcast.62), channel_id=1, replica_groups={{0,8,16,24,32,40,48,56,64,72,80,88,96,104,112,120,128,136,144,152,160,1..., dimensions={0} | all-to-all | bytes 1572864 | tf_op jit(solution)/shard_map/all_to_all | solution.py:52
  34.5 3.6 %shard_map.73 = bf16[4,256,1536]{2,1,0:T(8,128)(2,1)} custom-call(bf16[256,6144]{1,0:T(8,128)(2,1)} %bitcast.61), custom_call_target="tpu_custom_call" | custom-call | bytes 6291456 | tf_op jit(solution)/shard_map/pallas_call | solution.py:195
  38.1 3.7 %all-to-all-start.1 = ((bf16[4,256,1536]{2,1,0:T(8,128)(2,1)}), bf16[4,256,1536]{2,1,0:T(8,128)(2,1)S(1)}, u32[]{:S(2)}, u32[]{:S(2)}) async-start(bf16[4,256,1536]{2,1,0:T(8,128)(2,1)} %shard_map.73), calls=%async_computation.1 | async-start | bytes 6291456 | tf_op jit(solution)/shard_map/all_to_all | solution.py:52
  41.9 3.0 dynamic-slice_bitcast_fusion
  48.7 1.7 collective-permute-start.2
  50.4 53.3 %collective-permute-done.2 = bf16[768,256]{1,0:T(8,128)(2,1)S(1)} collective-permute-done((bf16[768,256]{1,0:T(8,128)(2,1)S(1)}, bf16[768,256]{1,0:T(8,128)(2,1)S(1)}, u32[]{:S(2)}, u32[]{:S(2)}) %collective-permute-start.2) | collective-permute-done | bytes 393248 | tf_op jit(solution)/shard_map/ppermute | solution.py:67
  104.4 4.6 %all-gather.2.cloned.1.call-done.rows_hbm = bf16[512,6144]{1,0:T(8,128)(2,1)} async-done(((bf16[64,6144]{1,0:T(8,128)(2,1)}), bf16[512,6144]{1,0:T(8,128)(2,1)}) %all-gather.2.cloned.1.call-update) | async-done | bytes 6291472 | tf_op jit(solution)/shard_map/all_gather | solution.py:311
  109.0 6.0 %shard_map.74.refs_0_ = bf16[512,256]{1,0:T(8,128)(2,1)S(1)} custom-call(bf16[512,6144]{1,0:T(8,128)(2,1)} %all-gather.2.cloned.1.call-done.rows_hbm, bf16[6144,256]{1,0:T(8,128)(2,1)} %bitcast.59, bf16[6144,256]{1,0:T(8,128)(2,1)} %bitcast.57), custom_call_target="tpu_custom_call" | custom-call | flops 3221225472 | bytes 12582912 | tf_op jit(solution)/shard_map/pallas_call | solution.py:159
  116.2 2.4 collective-permute-start.4
  119.8 3.6 %collective-permute-done.3.refs_1_ = bf16[512,256]{1,0:T(8,128)(2,1)S(1)} collective-permute-done((bf16[512,256]{1,0:T(8,128)(2,1)S(1)}, bf16[512,256]{1,0:T(8,128)(2,1)S(1)}, u32[]{:S(2)}, u32[]{:S(2)}) %collective-permute-start.3) | collective-permute-done | bytes 262176 | tf_op jit(solution)/shard_map/ppermute | solution.py:67
  123.4 6.6 %collective-permute-done.4.refs_2_ = bf16[512,256]{1,0:T(8,128)(2,1)S(1)} collective-permute-done((bf16[512,256]{1,0:T(8,128)(2,1)S(1)}, bf16[512,256]{1,0:T(8,128)(2,1)S(1)}, u32[]{:S(2)}, u32[]{:S(2)}) %collective-permute-start.4) | collective-permute-done | bytes 262176 | tf_op jit(solution)/shard_map/ppermute | solution.py:67
  130.0 3.3 shard_map.75
  133.3 40.9 %all_to_all.31.up_ref = bf16[4,1536,256]{2,1,0:T(8,128)(2,1)S(1)} all-to-all(bf16[4,1536,256]{2,1,0:T(8,128)(2,1)} %bitcast.58), channel_id=1, replica_groups={{0,8,16,24},{1,9,17,25},{2,10,18,26},{3,11,19,27},{4,12,20,28},{5,13,21..., dimensions={0} | all-to-all | bytes 6291456 | tf_op jit(solution)/shard_map/all_to_all | solution.py:52
  174.2 1.7 reshape.92
  175.9 7.1 %all-to-all-start.3 = ((bf16[32,2,1536]{2,1,0:T(2,128)(2,1)}), bf16[32,2,1536]{2,1,0:T(2,128)(2,1)S(1)}, u32[]{:S(2)}, u32[]{:S(2)}) async-start(bf16[32,2,1536]{2,1,0:T(2,128)(2,1)} %reshape.92), calls=%async_computation.4 | async-start | bytes 393216 | tf_op jit(solution)/shard_map/all_to_all | solution.py:52
  183.2 8.0 %all-to-all-done.3 = bf16[32,2,1536]{2,1,0:T(2,128)(2,1)S(1)} async-done(((bf16[32,2,1536]{2,1,0:T(2,128)(2,1)}), bf16[32,2,1536]{2,1,0:T(2,128)(2,1)S(1)}, u32[]{:S(2)}, u32[]{:S(2)}) %all-to-all-start.3) | async-done | bytes 196640 | tf_op jit(solution)/shard_map/all_to_all | solution.py:52
  192.9 12.1 %all_to_all.32 = bf16[32,2,1536]{2,1,0:T(2,128)(2,1)S(1)} all-to-all(bf16[32,2,1536]{2,1,0:T(2,128)(2,1)S(1)} %bitcast.66), channel_id=1, replica_groups={{0,8,16,24,32,40,48,56,64,72,80,88,96,104,112,120,128,136,144,152,160,1..., dimensions={0} | all-to-all | bytes 393216 | tf_op jit(solution)/shard_map/all_to_all | solution.py:52
  205.3 2.7 collective-permute-start.9
  208.0 4.5 %collective-permute-done.6 = bf16[64,1536]{1,0:T(8,128)(2,1)S(1)} collective-permute-done((bf16[64,1536]{1,0:T(8,128)(2,1)S(1)}, bf16[64,1536]{1,0:T(8,128)(2,1)S(1)}, u32[]{:S(2)}, u32[]{:S(2)}) %collective-permute-start.6) | collective-permute-done | bytes 196640 | tf_op jit(solution)/shard_map/ppermute | solution.py:67
  212.5 2.7 collective-permute-start.10
  215.1 3.6 %collective-permute-done.7 = bf16[64,1536]{1,0:T(8,128)(2,1)} collective-permute-done((bf16[64,1536]{1,0:T(8,128)(2,1)S(1)}, bf16[64,1536]{1,0:T(8,128)(2,1)}, u32[]{:S(2)}, u32[]{:S(2)}) %collective-permute-start.7) | collective-permute-done | bytes 196640 | tf_op jit(solution)/shard_map/ppermute | solution.py:67
  220.0 2.7 collective-permute-start.11
  222.7 2.0 collective-permute-done.8
  225.9 2.9 collective-permute-start.13
  230.8 1.8 shard_map.78
  232.6 1.9 fusion.22
  234.4 1.7 collective-permute-start.15
  236.1 1.4 copy-done.2
  237.5 3.0 shard_map.77
  240.6 2.6 collective-permute-start.17
  243.2 3.0 shard_map.79
  248.3 2.4 collective-permute-start.18
  253.2 1.8 shard_map.76
  255.0 3.2 collective-permute-done.16
  258.2 1.5 convert_add_fusion
  260.2 3.8 %collective-permute-start.20 = (bf16[512,256]{1,0:T(8,128)(2,1)S(1)}, bf16[512,256]{1,0:T(8,128)(2,1)S(1)}, u32[]{:S(2)}, u32[]{:S(2)}) collective-permute-start(bf16[512,256]{1,0:T(8,128)(2,1)S(1)} %fusion.9.refs_0_), channel_id=1, source_target_pairs={{0,16},{1,17},{2,18},{3,19},{4,20},{5,21},{6,22},{7,23},{8,24},{9,... | collective-permute-start | bytes 786440 | tf_op jit(solution)/shard_map/ppermute | solution.py:67
  264.1 2.5 collective-permute-done.19.refs_1_
  266.6 4.1 %collective-permute-done.20.refs_2_ = bf16[512,256]{1,0:T(8,128)(2,1)S(1)} collective-permute-done((bf16[512,256]{1,0:T(8,128)(2,1)S(1)}, bf16[512,256]{1,0:T(8,128)(2,1)S(1)}, u32[]{:S(2)}, u32[]{:S(2)}) %collective-permute-start.20) | collective-permute-done | bytes 262176 | tf_op jit(solution)/shard_map/ppermute | solution.py:67
  270.7 2.5 shard_map.80
  273.3 2.7 collective-permute-start.26
  276.0 2.0 collective-permute-done.22
  278.2 2.7 collective-permute-start.27
  280.9 2.9 collective-permute-done.23
  284.0 5.7 %collective-permute-done.24 = bf16[64,1536]{1,0:T(8,128)(2,1)S(1)} collective-permute-done((bf16[64,1536]{1,0:T(8,128)(2,1)S(1)}, bf16[64,1536]{1,0:T(8,128)(2,1)S(1)}, u32[]{:S(2)}, u32[]{:S(2)}) %collective-permute-start.24) | collective-permute-done | bytes 196640 | tf_op jit(solution)/shard_map/ppermute | solution.py:67
  291.4 3.1 collective-permute-done.28
  294.5 2.8 collective-permute-start.29
  297.3 2.6 collective-permute-done.29
  300.1 24.7 %all_to_all.33 = bf16[32,2,1536]{2,1,0:T(2,128)(2,1)S(1)} all-to-all(bf16[32,2,1536]{2,1,0:T(2,128)(2,1)S(1)} %reshape.101), channel_id=1, replica_groups={{0,8,16,24,32,40,48,56,64,72,80,88,96,104,112,120,128,136,144,152,160,1..., dimensions={0} | all-to-all | bytes 393216 | tf_op jit(solution)/shard_map/all_to_all | solution.py:52
  (136 shorter events, 27.9 us)
Async XLA Ops:
  6.5 102.4 %all-gather.2.cloned.1.call-start = ((), (), s32[]{:S(2)}) async-start(), calls=%async_computation.7 | async-start | bytes 7077888 | tf_op jit(solution)/shard_map/all_gather | solution.py:311
  38.1 66.3 %all-to-all-start.1 = ((bf16[4,256,1536]{2,1,0:T(8,128)(2,1)}), bf16[4,256,1536]{2,1,0:T(8,128)(2,1)S(1)}, u32[]{:S(2)}, u32[]{:S(2)}) async-start(bf16[4,256,1536]{2,1,0:T(8,128)(2,1)} %shard_map.73), calls=%async_computation.1 | async-start | bytes 6291456 | tf_op jit(solution)/shard_map/all_to_all | solution.py:52
  41.8 132.3 %reduce-scatter.2.cloned.1.call-start = ((), (), s32[]{:S(2)}) async-start(), calls=%async_computation.8 | async-start | bytes 1769472 | tf_op jit(solution)/shard_map/reduce_scatter | solution.py:317
  45.0 58.7 %collective-permute-start = (bf16[1536,256]{1,0:T(8,128)(2,1)}, bf16[1536,256]{1,0:T(8,128)(2,1)}, u32[]{:S(2)}, u32[]{:S(2)}) collective-permute-start(bf16[1536,256]{1,0:T(8,128)(2,1)} %get-tuple-element.35), channel_id=1, source_target_pairs={{0,8},{1,9},{2,10},{3,11},{4,12},{5,13},{6,14},{7,15},{8,16},{9,17... | collective-permute-start | bytes 2359304 | tf_op jit(solution)/shard_map/ppermute | solution.py:67
  46.3 58.1 %collective-permute-start.1 = (bf16[1536,256]{1,0:T(8,128)(2,1)}, bf16[1536,256]{1,0:T(8,128)(2,1)}, u32[]{:S(2)}, u32[]{:S(2)}) collective-permute-start(bf16[1536,256]{1,0:T(8,128)(2,1)} %get-tuple-element.34), channel_id=1, source_target_pairs={{0,24},{1,25},{2,26},{3,27},{4,28},{5,29},{6,30},{7,31},{8,0},{9,1... | collective-permute-start | bytes 2359304 | tf_op jit(solution)/shard_map/ppermute | solution.py:67
  48.7 55.0 %collective-permute-start.2 = (bf16[768,256]{1,0:T(8,128)(2,1)S(1)}, bf16[768,256]{1,0:T(8,128)(2,1)S(1)}, u32[]{:S(2)}, u32[]{:S(2)}) collective-permute-start(bf16[768,256]{1,0:T(8,128)(2,1)S(1)} %dynamic-slice_bitcast_fusion.3), channel_id=1, source_target_pairs={{0,16},{1,17},{2,18},{3,19},{4,20},{5,21},{6,22},{7,23},{8,24},{9,... | collective-permute-start | bytes 1179656 | tf_op jit(solution)/shard_map/ppermute | solution.py:67
  104.4 25.6 %copy-start.5 = (bf16[4,256,1536]{2,1,0:T(8,128)(2,1)}, bf16[4,256,1536]{2,1,0:T(8,128)(2,1)S(1)}, u32[]{:S(2)}) copy-start(bf16[4,256,1536]{2,1,0:T(8,128)(2,1)S(1)} %all-to-all-done.1.refs_4_) | copy-start | bytes 9437188
  114.9 8.5 %collective-permute-start.3 = (bf16[512,256]{1,0:T(8,128)(2,1)S(1)}, bf16[512,256]{1,0:T(8,128)(2,1)S(1)}, u32[]{:S(2)}, u32[]{:S(2)}) collective-permute-start(bf16[512,256]{1,0:T(8,128)(2,1)S(1)} %shard_map.74.refs_0_), channel_id=1, source_target_pairs={{0,8},{1,9},{2,10},{3,11},{4,12},{5,13},{6,14},{7,15},{8,16},{9,17... | collective-permute-start | bytes 786440 | tf_op jit(solution)/shard_map/ppermute | solution.py:67
  116.2 13.8 %collective-permute-start.4 = (bf16[512,256]{1,0:T(8,128)(2,1)S(1)}, bf16[512,256]{1,0:T(8,128)(2,1)S(1)}, u32[]{:S(2)}, u32[]{:S(2)}) collective-permute-start(bf16[512,256]{1,0:T(8,128)(2,1)S(1)} %shard_map.74.refs_0_), channel_id=1, source_target_pairs={{0,16},{1,17},{2,18},{3,19},{4,20},{5,21},{6,22},{7,23},{8,24},{9,... | collective-permute-start | bytes 786440 | tf_op jit(solution)/shard_map/ppermute | solution.py:67
  118.7 11.3 %collective-permute-start.5 = (bf16[512,256]{1,0:T(8,128)(2,1)S(1)}, bf16[512,256]{1,0:T(8,128)(2,1)S(1)}, u32[]{:S(2)}, u32[]{:S(2)}) collective-permute-start(bf16[512,256]{1,0:T(8,128)(2,1)S(1)} %shard_map.74.refs_0_), channel_id=1, source_target_pairs={{0,24},{1,25},{2,26},{3,27},{4,28},{5,29},{6,30},{7,31},{8,0},{9,1... | collective-permute-start | bytes 786440 | tf_op jit(solution)/shard_map/ppermute | solution.py:67
  133.3 58.0 %copy-start.10 = (bf16[4,6144]{1,0:T(4,128)(2,1)S(1)}, bf16[4,6144]{1,0:T(4,128)(2,1)}, u32[]{:S(2)}) copy-start(bf16[4,6144]{1,0:T(4,128)(2,1)} %param.7) | copy-start | bytes 147460
  174.2 18.2 %copy-start.19 = (f32[6144]{0:T(1024)S(1)}, f32[6144]{0:T(1024)}, u32[]{:S(2)}) copy-start(f32[6144]{0:T(1024)} %param.8) | copy-start | bytes 73732
  175.9 15.3 %all-to-all-start.3 = ((bf16[32,2,1536]{2,1,0:T(2,128)(2,1)}), bf16[32,2,1536]{2,1,0:T(2,128)(2,1)S(1)}, u32[]{:S(2)}, u32[]{:S(2)}) async-start(bf16[32,2,1536]{2,1,0:T(2,128)(2,1)} %reshape.92), calls=%async_computation.4 | async-start | bytes 393216 | tf_op jit(solution)/shard_map/all_to_all | solution.py:52
  205.1 7.4 %collective-permute-start.6 = (bf16[64,1536]{1,0:T(8,128)(2,1)S(1)}, bf16[64,1536]{1,0:T(8,128)(2,1)S(1)}, u32[]{:S(2)}, u32[]{:S(2)}) collective-permute-start(bf16[64,1536]{1,0:T(8,128)(2,1)S(1)} %reshape.97), channel_id=1, source_target_pairs={{0,1},{1,2},{2,3},{3,4},{4,5},{5,6},{6,7},{7,0},{8,9},{9,10},{10,1... | collective-permute-start | bytes 589832 | tf_op jit(solution)/shard_map/ppermute | solution.py:67
  205.3 7.1 %collective-permute-start.9 = (bf16[64,1536]{1,0:T(8,128)(2,1)S(1)}, bf16[64,1536]{1,0:T(8,128)(2,1)}, u32[]{:S(2)}, u32[]{:S(2)}) collective-permute-start(bf16[64,1536]{1,0:T(8,128)(2,1)S(1)} %reshape.97), channel_id=1, source_target_pairs={{0,7},{1,0},{2,1},{3,2},{4,3},{5,4},{6,5},{7,6},{8,15},{9,8},{10,9... | collective-permute-start | bytes 589832 | tf_op jit(solution)/shard_map/ppermute | solution.py:67
  212.5 2.7 copy-start.17
  212.5 6.3 %collective-permute-start.7 = (bf16[64,1536]{1,0:T(8,128)(2,1)S(1)}, bf16[64,1536]{1,0:T(8,128)(2,1)}, u32[]{:S(2)}, u32[]{:S(2)}) collective-permute-start(bf16[64,1536]{1,0:T(8,128)(2,1)S(1)} %collective-permute-done.6), channel_id=1, source_target_pairs={{0,1},{1,2},{2,3},{3,4},{4,5},{5,6},{6,7},{7,0},{8,9},{9,10},{10,1... | collective-permute-start | bytes 589832 | tf_op jit(solution)/shard_map/ppermute | solution.py:67
  212.5 7.5 %collective-permute-start.10 = (bf16[64,1536]{1,0:T(8,128)(2,1)}, bf16[64,1536]{1,0:T(8,128)(2,1)}, u32[]{:S(2)}, u32[]{:S(2)}) collective-permute-start(bf16[64,1536]{1,0:T(8,128)(2,1)} %collective-permute-done.9), channel_id=1, source_target_pairs={{0,7},{1,0},{2,1},{3,2},{4,3},{5,4},{6,5},{7,6},{8,15},{9,8},{10,9... | collective-permute-start | bytes 589832 | tf_op jit(solution)/shard_map/ppermute | solution.py:67
  218.8 5.9 %collective-permute-start.8 = (bf16[64,1536]{1,0:T(8,128)(2,1)}, bf16[64,1536]{1,0:T(8,128)(2,1)S(1)}, u32[]{:S(2)}, u32[]{:S(2)}) collective-permute-start(bf16[64,1536]{1,0:T(8,128)(2,1)} %collective-permute-done.7), channel_id=1, source_target_pairs={{0,1},{1,2},{2,3},{3,4},{4,5},{5,6},{6,7},{7,0},{8,9},{9,10},{10,1... | collective-permute-start | bytes 589832 | tf_op jit(solution)/shard_map/ppermute | solution.py:67
  218.8 7.0 %copy-start.18 = (bf16[64,1536]{1,0:T(8,128)(2,1)S(1)}, bf16[64,1536]{1,0:T(8,128)(2,1)}, u32[]{:S(2)}) copy-start(bf16[64,1536]{1,0:T(8,128)(2,1)} %copy-done.17) | copy-start | bytes 589828
  219.9 10.9 %collective-permute-start.14 = (bf16[768,256]{1,0:T(8,128)(2,1)S(1)}, bf16[768,256]{1,0:T(8,128)(2,1)S(1)}, u32[]{:S(2)}, u32[]{:S(2)}) collective-permute-start(bf16[768,256]{1,0:T(8,128)(2,1)S(1)} %constant_dynamic-slice_fusion), channel_id=1, source_target_pairs={{0,16},{1,17},{2,18},{3,19},{4,20},{5,21},{6,22},{7,23},{8,24},{9,... | collective-permute-start | bytes 1179656 | tf_op jit(solution)/shard_map/ppermute | solution.py:67
  220.0 5.9 %collective-permute-start.11 = (bf16[64,1536]{1,0:T(8,128)(2,1)}, bf16[64,1536]{1,0:T(8,128)(2,1)S(1)}, u32[]{:S(2)}, u32[]{:S(2)}) collective-permute-start(bf16[64,1536]{1,0:T(8,128)(2,1)} %collective-permute-done.10), channel_id=1, source_target_pairs={{0,7},{1,0},{2,1},{3,2},{4,3},{5,4},{6,5},{7,6},{8,15},{9,8},{10,9... | collective-permute-start | bytes 589832 | tf_op jit(solution)/shard_map/ppermute | solution.py:67
  224.7 6.0 %copy-start.13 = (bf16[768,256]{1,0:T(8,128)(2,1)S(1)}, bf16[768,256]{1,0:T(8,128)(2,1)}, u32[]{:S(2)}) copy-start(bf16[768,256]{1,0:T(8,128)(2,1)} %copy-done.12) | copy-start | bytes 1179652
  224.7 5.9 %collective-permute-start.12 = (bf16[32,1536]{1,0:T(8,128)(2,1)S(1)}, bf16[32,1536]{1,0:T(8,128)(2,1)S(1)}, u32[]{:S(2)}, u32[]{:S(2)}) collective-permute-start(bf16[32,1536]{1,0:T(8,128)(2,1)S(1)} %slice.113), channel_id=1, source_target_pairs={{0,1},{1,2},{2,3},{3,4},{4,5},{5,6},{6,7},{7,0},{8,9},{9,10},{10,1... | collective-permute-start | bytes 294920 | tf_op jit(solution)/shard_map/ppermute | solution.py:67
  225.9 4.8 %collective-permute-start.13 = (bf16[32,1536]{1,0:T(8,128)(2,1)S(1)}, bf16[32,1536]{1,0:T(8,128)(2,1)S(1)}, u32[]{:S(2)}, u32[]{:S(2)}) collective-permute-start(bf16[32,1536]{1,0:T(8,128)(2,1)S(1)} %slice.114), channel_id=1, source_target_pairs={{0,7},{1,0},{2,1},{3,2},{4,3},{5,4},{6,5},{7,6},{8,15},{9,8},{10,9... | collective-permute-start | bytes 294920 | tf_op jit(solution)/shard_map/ppermute | solution.py:67
  230.7 1.9 copy-start.1
  234.4 11.7 %collective-permute-start.15 = (bf16[256,512]{1,0:T(8,128)(2,1)}, bf16[256,512]{1,0:T(8,128)(2,1)S(1)}, u32[]{:S(2)}, u32[]{:S(2)}) collective-permute-start(bf16[256,512]{1,0:T(8,128)(2,1)} %get-tuple-element.44), channel_id=1, source_target_pairs={{0,8},{1,9},{2,10},{3,11},{4,12},{5,13},{6,14},{7,15},{8,16},{9,17... | collective-permute-start | bytes 786440 | tf_op jit(solution)/shard_map/ppermute | solution.py:67
  237.5 3.0 copy-start.16
  237.5 5.6 %copy-start.3 = (bf16[512,1536]{1,0:T(8,128)(2,1)S(1)}, bf16[512,1536]{1,0:T(8,128)(2,1)}, u32[]{:S(2)}) copy-start(bf16[512,1536]{1,0:T(8,128)(2,1)} %copy-done.1) | copy-start | bytes 4718596
  240.6 6.5 %collective-permute-start.17 = (bf16[256,512]{1,0:T(8,128)(2,1)S(1)}, bf16[256,512]{1,0:T(8,128)(2,1)S(1)}, u32[]{:S(2)}, u32[]{:S(2)}) collective-permute-start(bf16[256,512]{1,0:T(8,128)(2,1)S(1)} %copy-done.16), channel_id=1, source_target_pairs={{0,24},{1,25},{2,26},{3,27},{4,28},{5,29},{6,30},{7,31},{8,0},{9,1... | collective-permute-start | bytes 786440 | tf_op jit(solution)/shard_map/ppermute | solution.py:67
  243.2 3.0 copy-start.9
  243.2 3.1 slice-start.1
  247.1 11.1 %collective-permute-start.16 = (bf16[512,512]{1,0:T(8,128)(2,1)}, bf16[512,512]{1,0:T(8,128)(2,1)}, u32[]{:S(2)}, u32[]{:S(2)}) collective-permute-start(bf16[512,512]{1,0:T(8,128)(2,1)} %pad_maximum_fusion.1), channel_id=1, source_target_pairs={{0,8},{1,9},{2,10},{3,11},{4,12},{5,13},{6,14},{7,15},{8,16},{9,17... | collective-permute-start | bytes 1572872 | tf_op jit(solution)/shard_map/ppermute | solution.py:67
  248.3 9.9 %collective-permute-start.18 = (bf16[512,512]{1,0:T(8,128)(2,1)}, bf16[512,512]{1,0:T(8,128)(2,1)}, u32[]{:S(2)}, u32[]{:S(2)}) collective-permute-start(bf16[512,512]{1,0:T(8,128)(2,1)} %pad_maximum_fusion.2), channel_id=1, source_target_pairs={{0,24},{1,25},{2,26},{3,27},{4,28},{5,29},{6,30},{7,31},{8,0},{9,1... | collective-permute-start | bytes 1572872 | tf_op jit(solution)/shard_map/ppermute | solution.py:67
  255.0 15.7 %copy-start.6 = (bf16[4,256,1536]{2,1,0:T(8,128)(2,1)S(1)}, bf16[4,256,1536]{2,1,0:T(8,128)(2,1)}, u32[]{:S(2)}) copy-start(bf16[4,256,1536]{2,1,0:T(8,128)(2,1)} %copy-done.5) | copy-start | bytes 9437188
  259.9 6.7 %collective-permute-start.19 = (bf16[512,256]{1,0:T(8,128)(2,1)S(1)}, bf16[512,256]{1,0:T(8,128)(2,1)S(1)}, u32[]{:S(2)}, u32[]{:S(2)}) collective-permute-start(bf16[512,256]{1,0:T(8,128)(2,1)S(1)} %fusion.9.refs_0_), channel_id=1, source_target_pairs={{0,8},{1,9},{2,10},{3,11},{4,12},{5,13},{6,14},{7,15},{8,16},{9,17... | collective-permute-start | bytes 786440 | tf_op jit(solution)/shard_map/ppermute | solution.py:67
  260.2 10.5 %collective-permute-start.20 = (bf16[512,256]{1,0:T(8,128)(2,1)S(1)}, bf16[512,256]{1,0:T(8,128)(2,1)S(1)}, u32[]{:S(2)}, u32[]{:S(2)}) collective-permute-start(bf16[512,256]{1,0:T(8,128)(2,1)S(1)} %fusion.9.refs_0_), channel_id=1, source_target_pairs={{0,16},{1,17},{2,18},{3,19},{4,20},{5,21},{6,22},{7,23},{8,24},{9,... | collective-permute-start | bytes 786440 | tf_op jit(solution)/shard_map/ppermute | solution.py:67
  264.0 6.7 %collective-permute-start.21 = (bf16[512,256]{1,0:T(8,128)(2,1)S(1)}, bf16[512,256]{1,0:T(8,128)(2,1)S(1)}, u32[]{:S(2)}, u32[]{:S(2)}) collective-permute-start(bf16[512,256]{1,0:T(8,128)(2,1)S(1)} %fusion.9.refs_0_), channel_id=1, source_target_pairs={{0,24},{1,25},{2,26},{3,27},{4,28},{5,29},{6,30},{7,31},{8,0},{9,1... | collective-permute-start | bytes 786440 | tf_op jit(solution)/shard_map/ppermute | solution.py:67
  273.2 4.8 %collective-permute-start.22 = (bf16[32,1536]{1,0:T(8,128)(2,1)S(1)}, bf16[32,1536]{1,0:T(8,128)(2,1)S(1)}, u32[]{:S(2)}, u32[]{:S(2)}) collective-permute-start(bf16[32,1536]{1,0:T(8,128)(2,1)S(1)} %get-tuple-element.40), channel_id=1, source_target_pairs={{0,1},{1,2},{2,3},{3,4},{4,5},{5,6},{6,7},{7,0},{8,9},{9,10},{10,1... | collective-permute-start | bytes 294920 | tf_op jit(solution)/shard_map/ppermute | solution.py:67
  273.3 4.7 %collective-permute-start.26 = (bf16[32,1536]{1,0:T(8,128)(2,1)S(1)}, bf16[32,1536]{1,0:T(8,128)(2,1)S(1)}, u32[]{:S(2)}, u32[]{:S(2)}) collective-permute-start(bf16[32,1536]{1,0:T(8,128)(2,1)S(1)} %get-tuple-element.41), channel_id=1, source_target_pairs={{0,7},{1,0},{2,1},{3,2},{4,3},{5,4},{6,5},{7,6},{8,15},{9,8},{10,9... | collective-permute-start | bytes 294920 | tf_op jit(solution)/shard_map/ppermute | solution.py:67
  278.0 5.8 %collective-permute-start.23 = (bf16[64,1536]{1,0:T(8,128)(2,1)S(1)}, bf16[64,1536]{1,0:T(8,128)(2,1)S(1)}, u32[]{:S(2)}, u32[]{:S(2)}) collective-permute-start(bf16[64,1536]{1,0:T(8,128)(2,1)S(1)} %pad_maximum_fusion.3), channel_id=1, source_target_pairs={{0,1},{1,2},{2,3},{3,4},{4,5},{5,6},{6,7},{7,0},{8,9},{9,10},{10,1... | collective-permute-start | bytes 589832 | tf_op jit(solution)/shard_map/ppermute | solution.py:67
  278.2 5.8 %collective-permute-start.27 = (bf16[64,1536]{1,0:T(8,128)(2,1)S(1)}, bf16[64,1536]{1,0:T(8,128)(2,1)S(1)}, u32[]{:S(2)}, u32[]{:S(2)}) collective-permute-start(bf16[64,1536]{1,0:T(8,128)(2,1)S(1)} %pad_maximum_fusion.4), channel_id=1, source_target_pairs={{0,7},{1,0},{2,1},{3,2},{4,3},{5,4},{6,5},{7,6},{8,15},{9,8},{10,9... | collective-permute-start | bytes 589832 | tf_op jit(solution)/shard_map/ppermute | solution.py:67
  283.9 5.8 %collective-permute-start.24 = (bf16[64,1536]{1,0:T(8,128)(2,1)S(1)}, bf16[64,1536]{1,0:T(8,128)(2,1)S(1)}, u32[]{:S(2)}, u32[]{:S(2)}) collective-permute-start(bf16[64,1536]{1,0:T(8,128)(2,1)S(1)} %add_convert_fusion.6), channel_id=1, source_target_pairs={{0,1},{1,2},{2,3},{3,4},{4,5},{5,6},{6,7},{7,0},{8,9},{9,10},{10,1... | collective-permute-start | bytes 589832 | tf_op jit(solution)/shard_map/ppermute | solution.py:67
  289.8 35.0 %copy-start.11 = (bf16[4,6144]{1,0:T(4,128)(2,1)S(1)}, bf16[4,6144]{1,0:T(4,128)(2,1)}, u32[]{:S(2)}) copy-start(bf16[4,6144]{1,0:T(4,128)(2,1)} %param.7) | copy-start | bytes 147460
  289.8 35.0 %copy-start.15 = (f32[4,6144]{1,0:T(4,128)S(1)}, f32[4,6144]{1,0:T(4,128)}, u32[]{:S(2)}) copy-start(f32[4,6144]{1,0:T(4,128)} %copy-done.14) | copy-start | bytes 294916
  289.8 4.6 %collective-permute-start.28 = (bf16[64,1536]{1,0:T(8,128)(2,1)S(1)}, bf16[64,1536]{1,0:T(8,128)(2,1)S(1)}, u32[]{:S(2)}, u32[]{:S(2)}) collective-permute-start(bf16[64,1536]{1,0:T(8,128)(2,1)S(1)} %get-tuple-element.37), channel_id=1, source_target_pairs={{0,7},{1,0},{2,1},{3,2},{4,3},{5,4},{6,5},{7,6},{8,15},{9,8},{10,9... | collective-permute-start | bytes 589832 | tf_op jit(solution)/shard_map/ppermute | solution.py:67
  290.2 7.1 %collective-permute-start.25 = (bf16[64,1536]{1,0:T(8,128)(2,1)S(1)}, bf16[64,1536]{1,0:T(8,128)(2,1)S(1)}, u32[]{:S(2)}, u32[]{:S(2)}) collective-permute-start(bf16[64,1536]{1,0:T(8,128)(2,1)S(1)} %get-tuple-element.36), channel_id=1, source_target_pairs={{0,1},{1,2},{2,3},{3,4},{4,5},{5,6},{6,7},{7,0},{8,9},{9,10},{10,1... | collective-permute-start | bytes 589832 | tf_op jit(solution)/shard_map/ppermute | solution.py:67
  294.5 5.4 %collective-permute-start.29 = (bf16[64,1536]{1,0:T(8,128)(2,1)S(1)}, bf16[64,1536]{1,0:T(8,128)(2,1)S(1)}, u32[]{:S(2)}, u32[]{:S(2)}) collective-permute-start(bf16[64,1536]{1,0:T(8,128)(2,1)S(1)} %add_convert_fusion.3), channel_id=1, source_target_pairs={{0,7},{1,0},{2,1},{3,2},{4,3},{5,4},{6,5},{7,6},{8,15},{9,8},{10,9... | collective-permute-start | bytes 589832 | tf_op jit(solution)/shard_map/ppermute | solution.py:67
  (8 other events, 8.4 us)
Sparse Core Ops, SparseCore 0:
  34.6 74.2 all-gather.1
  133.4 35.4 reduce-scatter.1
